TPU v7x, 32 devices: a whole 2x2x4 slice. The times are simulated.
32 devices in a mesh: row: 8 (over z, y), col: 4 (over x, core).
Axes of the slice: x: 2, y: 2, z: 4, core: 2. Of those that a mesh axis runs over, the one named last changes fastest.
Arguments:
- water_depth: float32 [512, 512], P('row', 'col'), may hold values from 1 to 2
- discharge: float32 [2, 512, 512], P(None, 'row', 'col'), may hold values from -1.5 to 1.5
- sediment: float32 [4, 512, 512], P(None, 'row', 'col'), may hold values from 0.01 to 0.1
- bed_level: float32 [128, 128], P(('row', 'col')), may hold values from -3 to 3
- cell_map: int32 [512, 512], P('row', 'col'), may hold values from 0 to 2047, as said below
- wet_mask: int32 [512, 512], P('row', 'col'), may hold values 0 or 1
- sediment_params: float32 [3, 4], replicated, may hold values from 0.5 to 2
Outputs:
- depth_out: float32 [512, 512], P('row', 'col')
- discharge_out: float32 [2, 512, 512], P(None, 'row', 'col')
- sediment_out: float32 [4, 512, 512], P(None, 'row', 'col')
- fine_bed: float32 [512, 512], P('row', 'col')
- bed_out: float32 [128, 128], P(('row', 'col'))
- deposit: float32 [4, 128, 128], P(None, ('row', 'col'))
Inputs may be any that keep to these rules, and one draw needn't show every extreme that they name: cell_map[i, j] = r * 128 + c with r within 1 of (i % 64) // 4 and 0 <= r < 16, and c within 3 of j // 4.
All inputs are finite; a program needn't handle non-finite values. No bound on the sum of `wet_mask` on one device may be relied on, other than what follows from the above.
Results may differ from a plain program's by a relative error of at most 0.0003.
Values sent between devices are 32-bit elements; how exact they have to be, the bound alone decides.
No kernel may reach another device: no remote copies, remote signals or barrier semaphores. Data moves between devices by JAX's collectives and lax.ppermute only.
A program may use at most 64 MiB of HBM per device.

v0:
```python
import functools

import jax
import jax.numpy as jnp
from jax import lax
from jax.experimental import pallas as pl
from jax.experimental.pallas import tpu as pltpu
from jax.sharding import PartitionSpec as P

SUBSTEPS = 4
LANES = 128
SUB = 8
RIM = 2 * SUBSTEPS

gravity = 1.0
time_step = 0.2
depth_floor = 1.25
drag_coeff = 0.02
settle_base = 0.05
critical_base = 0.05
erode_base = 0.002
exner_factor = 400.0


def vmem():
    return pl.BlockSpec(memory_space=pltpu.VMEM)


def smem():
    return pl.BlockSpec(memory_space=pltpu.SMEM)


def lane_ids(shape):
    return lax.broadcasted_iota(jnp.int32, shape, len(shape) - 1)


def pick(table, index):
    return jnp.take_along_axis(table, index, axis=1, mode="promise_in_bounds")


def planes_of(depth, flow, mud, wet, cells):
    out = [lambda r: depth[r, :]]
    out += [lambda r, k=k: flow[k, r, :] for k in range(flow.shape[0])]
    out += [lambda r, k=k: mud[k, r, :] for k in range(mud.shape[0])]
    out += [lambda r: wet[r, :].astype(jnp.float32)]
    out += [lambda r: cells[r, :].astype(jnp.float32)]
    return out


def pack_kernel(depth, flow, mud, wet, cells, strip, out):
    rows = depth.shape[0]
    planes = planes_of(depth, flow, mud, wet, cells)
    group = lane_ids((SUB, LANES)) // RIM
    for start in range(0, rows, SUB):
        at = pl.ds(start, SUB)
        low = jnp.zeros((SUB, LANES), jnp.float32)
        high = low
        for p, plane in enumerate(planes):
            x = plane(at)
            low = jnp.where(group == p, pltpu.roll(x, RIM * p, 1) if p else x, low)
            high = jnp.where(group == p, pltpu.roll(x, (RIM * p + RIM) % LANES, 1), high)
        out[at, :] = low
        out[pl.ds(rows + start, SUB), :] = high
    strip_rows = strip.shape[0]
    for chunk in range(strip.shape[1] // LANES):
        out[pl.ds(2 * rows + chunk * strip_rows, strip_rows), :] = strip[
            :, chunk * LANES : (chunk + 1) * LANES
        ]


def spread_rows(frame_ref, block, shift):
    first = SUB + block * (SUB // 4) + shift
    low = jnp.broadcast_to(frame_ref[pl.ds(first, 1), :], (SUB, LANES))
    high = jnp.broadcast_to(frame_ref[pl.ds(first + 1, 1), :], (SUB, LANES))
    sub = lax.broadcasted_iota(jnp.int32, (SUB, LANES), 0)
    return jnp.where(sub < 4, low, high)


def split_cells(cells, band_cols):
    row = jnp.floor((cells + 0.5) * (1.0 / band_cols))
    return row.astype(jnp.int32), (cells - row * band_cols).astype(jnp.int32)


def row_shift_of(cell_row, block):
    sub = lax.broadcasted_iota(jnp.int32, (SUB, LANES), 0)
    return cell_row - (block * (SUB // 4) + sub // 4)


def lookup(frame_ref, block, shift, column):
    found = pick(spread_rows(frame_ref, block, 0), column)
    below = pick(spread_rows(frame_ref, block, -1), column)
    above = pick(spread_rows(frame_ref, block, 1), column)
    return jnp.where(shift == 0, found, jnp.where(shift < 0, below, above))


def fill_frame(frame_ref, band_rows, rows_of):
    frame_ref[...] = jnp.zeros_like(frame_ref)
    for r0, value in rows_of:
        frame_ref[pl.ds(SUB + r0, value.shape[0]), :] = value


def mid_kernel(
    geometry, depth, flow, mud, wet, cells, packs, frame, place,
    side, bed, code, send_a, send_b, frame_ref,
):
    rows = depth.shape[0]
    fractions = mud.shape[0]
    band_cols, cols_count, strip_rows, from_packs = geometry
    row_at, col_at, frame_start = place[0], place[1], place[2]
    coarse_start = place[3]
    if from_packs:
        fill_frame(
            frame_ref, None,
            [(d * strip_rows, packs[d, pl.ds(2 * rows, strip_rows), :]) for d in range(cols_count)],
        )
    else:
        fill_frame(frame_ref, None, [(0, frame[...])])
    lane = lane_ids((SUB, LANES))
    width = 4 * RIM
    inside = lane % width
    group = lane // width
    is_low = inside < RIM
    is_high = inside >= 3 * RIM
    own_index = jnp.where(
        is_low | is_high, 0, jnp.where(inside < 2 * RIM, inside - RIM, inside - 2 * RIM + LANES - RIM)
    )
    has_low = jnp.where(col_at > 0, 1.0, 0.0)
    has_high = jnp.where(col_at < cols_count - 1, 1.0, 0.0)
    scale = jnp.where(is_low, has_low, jnp.where(is_high, has_high, 1.0))
    left = jnp.maximum(col_at - 1, 0)
    right = jnp.minimum(col_at + 1, cols_count - 1)
    planes = planes_of(depth, flow, mud, wet, cells)
    count = len(planes)
    wet_at, cell_at = count - 2, count - 1
    parity = row_at % 2
    for block in range(rows // SUB):
        at = pl.ds(block * SUB, SUB)
        from_left = packs[left, pl.ds(rows + block * SUB, SUB), :]
        from_right = packs[right, pl.ds(block * SUB, SUB), :]

        def side_of(own, p):
            index = p * RIM + lane % RIM
            x = jnp.where(is_low, pick(from_left, index), jnp.where(is_high, pick(from_right, index), own))
            return x * scale

        def own_of(p):
            return pick(planes[p](at), own_index)

        sides = [side_of(own_of(p), p) for p in range(3)]
        own = own_of(3)
        for k in range(1, fractions):
            own = jnp.where(group == k, own_of(3 + k), own)
        sides.append(side_of(own, 3 + group))
        sides.append(side_of(own_of(wet_at), wet_at))
        side_row, side_col = split_cells(side_of(own_of(cell_at), cell_at), band_cols)
        side_at = jnp.where(scale > 0.0, side_col - frame_start, 0)
        sides.append(lookup(frame_ref, block, row_shift_of(side_row, block), side_at) * scale)
        cell_row, cell_col = split_cells(cells[at, :].astype(jnp.float32), band_cols)
        shift = row_shift_of(cell_row, block)
        bed_here = lookup(frame_ref, block, shift, cell_col - frame_start)
        bed[at, :] = bed_here
        code[at, :] = (shift + 1) * 7 + (cell_col - coarse_start - lane // 4 + 3)
        for p, x in enumerate(sides):
            side[p, at, :] = x
        edge = [planes[p](at) for p in range(count - 1)] + [bed_here] + sides

        def write(out):
            for p, x in enumerate(edge):
                out[p, :, :] = x

        if block == 0:
            pl.when(parity == 1)(lambda: write(send_a))
            pl.when(parity == 0)(lambda: write(send_b))
        if block == rows // SUB - 1:
            pl.when(parity == 0)(lambda: write(send_a))
            pl.when(parity == 1)(lambda: write(send_b))


def half_minmod(before, here, after):
    low = 0.5 * (here - before)
    high = 0.5 * (after - here)
    return jnp.maximum(jnp.minimum(low, high), jnp.minimum(jnp.maximum(low, high), 0.0))


def face_fluxes(lefts, rights, normal, half_open):
    speed_l = lefts[normal] * pl.reciprocal(jnp.maximum(lefts[0], depth_floor))
    speed_r = rights[normal] * pl.reciprocal(jnp.maximum(rights[0], depth_floor))
    wave = jnp.maximum(
        jnp.abs(speed_l) + jnp.sqrt(gravity * lefts[0]), jnp.abs(speed_r) + jnp.sqrt(gravity * rights[0])
    )
    to_l = half_open * (speed_l + wave)
    to_r = half_open * (speed_r - wave)
    out = [l * to_l + r * to_r for l, r in zip(lefts, rights)]
    out[normal] = out[normal] + (0.5 * gravity) * half_open * (lefts[0] * lefts[0] + rights[0] * rights[0])
    return out


def flow_kernel(
    depth, flow, mud, wet, bed, side, code, params, place, recv_a, recv_b,
    depth_out, flow_out, mud_out, partial,
    q_main, q_side, static_main, static_side, slope_main, slope_side, flux_main, flux_side, exchanged, code_ref,
):
    rows = depth.shape[0]
    fractions = mud.shape[0]
    channels = 3 + fractions
    top = SUB
    body = top + RIM
    blocks = (rows + 2 * RIM) // SUB
    parity = place[0] % 2
    lane = lane_ids((SUB, LANES))
    width = 4 * RIM
    group = lane // width

    main_planes = [depth] + [flow.at[k] for k in range(2)] + [mud.at[k] for k in range(fractions)]
    wet_main, bed_main = 0, 1

    def fill(dst, p_dst, own, p_recv):
        dst[p_dst, pl.ds(body, rows), :] = own
        a, b = recv_a[p_recv], recv_b[p_recv]
        dst[p_dst, pl.ds(top, RIM), :] = jnp.where(parity == 1, a, b)
        dst[p_dst, pl.ds(body + rows, RIM), :] = jnp.where(parity == 1, b, a)

    for k in range(channels):
        fill(q_main.at[0], k, main_planes[k][...], k)
    fill(static_main, wet_main, wet[...].astype(jnp.float32), channels)
    fill(static_main, bed_main, bed[...], channels + 1)
    for k in range(4):
        fill(q_side.at[0], k, side[k], channels + 2 + k)
    fill(static_side, wet_main, side[4], channels + 6)
    fill(static_side, bed_main, side[5], channels + 7)

    settle = [[settle_base * params[0, k] for k in range(fractions)]]
    inv_crit = [[1.0 / (critical_base * params[1, k]) for k in range(fractions)]]
    erode = [[erode_base * params[2, k] for k in range(fractions)]]

    def by_group(values):
        out = jnp.full((SUB, LANES), values[0], jnp.float32)
        for k in range(1, fractions):
            out = jnp.where(group == k, values[k], out)
        return out

    side_coeffs = ([by_group(settle[0])], [by_group(inv_crit[0])], [by_group(erode[0])])
    main_coeffs = (settle[0], inv_crit[0], erode[0])

    def edge_fix(k):
        g = (k - 3) if k >= 3 else 0
        return jnp.where(lane == 0, g * width + RIM - 1, jnp.where(lane == LANES - 1, g * width + 3 * RIM, 0))

    def flux_fix(k):
        g = (k - 3) if k >= 3 else 0
        return jnp.where(lane == 0, g * width + RIM - 1, jnp.where(lane == LANES - 1, g * width + 3 * RIM - 1, 0))

    edge_index = [edge_fix(max(k, 3)) for k in range(3, 3 + fractions)]
    flux_index = [flux_fix(max(k, 3)) for k in range(3, 3 + fractions)]
    first_lane = lane == 0
    last_lane = lane == LANES - 1

    def rows_at(ref, p, row):
        return ref[p, pl.ds(row, SUB), :]

    def statics(block, carry):
        r0 = pl.multiple_of(top + block * SUB, SUB)
        for ref, is_main in ((static_side, False), (static_main, True)):
            w = rows_at(ref, wet_main, r0)
            b_plus = rows_at(ref, bed_main, r0 + 1)
            b_minus = rows_at(ref, bed_main, r0 - 1)
            b = rows_at(ref, bed_main, r0)
            w_right, b_right = pltpu.roll(w, LANES - 1, 1), pltpu.roll(b, LANES - 1, 1)
            b_left = pltpu.roll(b, 1, 1)
            if is_main:
                w_edge = pick(rows_at(static_side, wet_main, r0), edge_index[0])
                b_edge = pick(rows_at(static_side, bed_main, r0), edge_index[0])
                w_right = jnp.where(last_lane, w_edge, w_right)
                b_right = jnp.where(last_lane, b_edge, b_right)
                b_left = jnp.where(first_lane, b_edge, b_left)
            at = pl.ds(r0, SUB)
            ref[2, at, :] = 0.5 * (w * rows_at(ref, wet_main, r0 + 1))
            ref[3, at, :] = 0.5 * (w * w_right)
            ref[4, at, :] = (0.5 * gravity) * (b_plus - b_minus)
            ref[5, at, :] = (0.5 * gravity) * (b_right - b_left)
            ref[6, at, :] = time_step * w
        return carry

    lax.fori_loop(0, blocks, statics, 0)

    def slopes(block, level):
        r0 = pl.multiple_of(top + block * SUB, SUB)
        at = pl.ds(r0, SUB)
        for q, s, n in ((q_side, slope_side, 4), (q_main, slope_main, channels)):
            if n == 4 and level == SUBSTEPS - 1:
                continue
            q = q.at[level % 2]
            for k in range(n):
                s[k, at, :] = half_minmod(rows_at(q, k, r0 - 1), rows_at(q, k, r0), rows_at(q, k, r0 + 1))

    def row_fluxes(q, s, f, static, n, r0):
        lefts = [rows_at(q, k, r0) + rows_at(s, k, r0) for k in range(n)]
        rights = [rows_at(q, k, r0 + 1) - rows_at(s, k, r0 + 1) for k in range(n)]
        out = face_fluxes(lefts, rights, 1, rows_at(static, 2, r0))
        for k in range(n):
            f[k, pl.ds(r0, SUB), :] = out[k]
        return [rows_at(f, k, r0 - 1) - out[k] for k in range(n)]

    def col_fluxes(here, static, n, r0, edges):
        lefts, rights = [], []
        for k in range(n):
            before, after = pltpu.roll(here[k], 1, 1), pltpu.roll(here[k], LANES - 1, 1)
            if edges is not None:
                edge = pick(edges[min(k, 3)], edge_index[max(k - 3, 0)])
                before = jnp.where(first_lane, edge, before)
                after = jnp.where(last_lane, edge, after)
            s = half_minmod(before, here[k], after)
            lefts.append(here[k] + s)
            rights.append(pltpu.roll(here[k] - s, LANES - 1, 1))
        return face_fluxes(lefts, rights, 2, rows_at(static, 3, r0))

    def update(here, net, static, coeffs, r0):
        step = rows_at(static, 6, r0)
        inv = pl.reciprocal(jnp.maximum(here[0], depth_floor))
        u, v = here[1] * inv, here[2] * inv
        squared = u * u + v * v + 1e-06
        drag = drag_coeff * jnp.sqrt(squared)
        new = [
            here[0] + step * net[0],
            here[1] + step * (net[1] - here[0] * rows_at(static, 4, r0) - drag * u),
            here[2] + step * (net[2] - here[0] * rows_at(static, 5, r0) - drag * v),
        ]
        changes = []
        for k in range(len(here) - 3):
            m = here[3 + k]
            settled = coeffs[0][k] * m * inv
            eroded = coeffs[2][k] * jnp.maximum(squared * coeffs[1][k] - 1.0, 0.0)
            change = step * (settled - eroded)
            changes.append(change)
            new.append(m + step * net[3 + k] - change)
        return new, changes

    def advance(block, level, rows_only=False):
        r0 = pl.multiple_of(top + block * SUB, SUB)
        at = pl.ds(r0, SUB)
        last = level == SUBSTEPS - 1
        qs, qm = q_side.at[level % 2], q_main.at[level % 2]
        if rows_only:
            row_fluxes(qm, slope_main, flux_main, static_main, channels, r0)
            return
        edges = [rows_at(qs, k, r0) for k in range(4)]
        side_flux = col_fluxes(edges, static_side, 4, r0, None)
        if not last:
            net = row_fluxes(qs, slope_side, flux_side, static_side, 4, r0)
            net = [x + (pltpu.roll(f, 1, 1) - f) for x, f in zip(net, side_flux)]
            new, _ = update(edges, net, static_side, side_coeffs, r0)
            for k in range(4):
                q_side[(level + 1) % 2, k, at, :] = new[k]
        net = row_fluxes(qm, slope_main, flux_main, static_main, channels, r0)
        here = [rows_at(qm, k, r0) for k in range(channels)]
        fluxes = col_fluxes(here, static_main, channels, r0, edges)
        for k in range(channels):
            edge = pick(side_flux[min(k, 3)], flux_index[max(k - 3, 0)])
            f = jnp.where(last_lane, edge, fluxes[k])
            net[k] = net[k] + (jnp.where(first_lane, edge, pltpu.roll(fluxes[k], 1, 1)) - f)
        new, changes = update(here, net, static_main, main_coeffs, r0)
        if last:
            out = pl.ds(pl.multiple_of(r0 - body, SUB), SUB)
            depth_out[out, :] = new[0]
            flow_out[0, out, :] = new[1]
            flow_out[1, out, :] = new[2]
            for k in range(fractions):
                mud_out[k, out, :] = new[3 + k]
        else:
            for k in range(channels):
                q_main[(level + 1) % 2, k, at, :] = new[k]
        for k in range(fractions):
            if level == 0:
                exchanged[k, at, :] = changes[k]
            else:
                exchanged[k, at, :] = exchanged[k, at, :] + changes[k]

    for level in range(SUBSTEPS):
        last = level == SUBSTEPS - 1

        def slope_step(block, carry, level=level):
            slopes(block, level)
            return carry

        def advance_step(block, carry, level=level):
            advance(block, level)
            return carry

        lax.fori_loop(0, blocks, slope_step, 0)
        if last:
            advance(0, level, rows_only=True)
            lax.fori_loop(1, blocks - 1, advance_step, 0)
        else:
            lax.fori_loop(0, blocks, advance_step, 0)

    coarse_rows = rows // 4
    code_ref[...] = code[...]
    parts = [[exchanged[f, pl.ds(body + k, coarse_rows, stride=4), :] for k in range(4)] for f in range(fractions)]
    codes = [code_ref[pl.ds(k, coarse_rows, stride=4), :] for k in range(4)]
    to_coarse = (
        lax.broadcasted_iota(jnp.int32, (LANES, LANES), 0) // 4 == lax.broadcasted_iota(jnp.int32, (LANES, LANES), 1)
    ).astype(jnp.float32)
    total = None
    for col_shift in range(7):
        sums = [None] * fractions
        for row_shift in range(3):
            hits = [c == row_shift * 7 + col_shift for c in codes]
            for f in range(fractions):
                part = None
                for k in range(4):
                    x = jnp.where(hits[k], parts[f][k], 0.0)
                    part = x if part is None else part + x
                if row_shift != 1:
                    part = pltpu.roll(part, 1 if row_shift == 2 else coarse_rows - 1, 0)
                sums[f] = part if sums[f] is None else sums[f] + part
        z = jnp.dot(
            jnp.concatenate(sums, axis=0), to_coarse, precision=lax.Precision.HIGHEST,
            preferred_element_type=jnp.float32,
        )
        z = pltpu.roll(z, (place[3] - place[2] + col_shift - 3 + LANES) % LANES, 1)
        total = z if total is None else total + z
    partial[...] = total


def bed_kernel(geometry, sums, bed, cells, place, bed_out, deposit_out, fine, frame_ref, total_ref):
    band_cols, cols_count, strip_rows = geometry
    rows = cells.shape[0]
    band_rows = rows // 4
    fractions = sums.shape[1] // band_rows
    total = sums[0]
    for d in range(1, cols_count):
        total = total + sums[d]
    total_ref[...] = (exner_factor / 16.0) * total
    at = place[1] * strip_rows
    frame_ref[...] = jnp.zeros_like(frame_ref)
    whole = None
    for f in range(fractions):
        part = total_ref[pl.ds(f * band_rows, band_rows), :]
        whole = part if whole is None else whole + part
        deposit_out[f, :, :] = total_ref[pl.ds(f * band_rows + at, strip_rows), :]
    frame_ref[pl.ds(SUB, band_rows), :] = bed[pl.ds(SUB, band_rows), :] + whole
    bed_out[...] = frame_ref[pl.ds(SUB + at, strip_rows), :]
    for block in range(rows // SUB):
        here = pl.ds(block * SUB, SUB)
        cell_row, cell_col = split_cells(cells[here, :].astype(jnp.float32), band_cols)
        fine[here, :] = lookup(frame_ref, block, row_shift_of(cell_row, block), cell_col)


def local(water_depth, discharge, sediment, bed_level, cell_map, wet_mask, sediment_params):
    tile_rows, tile_cols = water_depth.shape
    fractions = sediment.shape[0]
    strip_rows, band_cols = bed_level.shape
    cols_count = lax.axis_size("col")
    rows_count = lax.axis_size("row")
    band_rows = tile_rows // 4
    f32 = functools.partial(jax.ShapeDtypeStruct, dtype=jnp.float32)
    row_at, col_at = lax.axis_index("row"), lax.axis_index("col")
    coarse_start = col_at * (tile_cols // 4)
    narrow = band_cols == LANES
    frame_start = 0 * coarse_start if narrow else coarse_start - (LANES - tile_cols // 4) // 2
    place = jnp.stack([row_at, col_at, frame_start, coarse_start]).astype(jnp.int32)
    chunks = band_cols // LANES
    pack_rows = 2 * tile_rows + -(-chunks * strip_rows // SUB) * SUB

    packed = pl.pallas_call(
        pack_kernel, out_shape=f32((pack_rows, LANES)), in_specs=[vmem()] * 6, out_specs=vmem(),
    )(water_depth, discharge, sediment, wet_mask, cell_map, bed_level)
    packs = lax.all_gather(packed, "col", axis=0)

    if narrow:
        frame = jnp.zeros((SUB, LANES), jnp.float32)
    else:
        strips = packs[:, 2 * tile_rows : 2 * tile_rows + chunks * strip_rows]
        band = strips.reshape(cols_count, chunks, strip_rows, LANES).transpose(0, 2, 1, 3).reshape(band_rows, band_cols)
        wide = jnp.pad(band, ((0, 0), (LANES, LANES)))
        frame = lax.dynamic_slice(wide, (jnp.int32(0), frame_start + LANES), (band_rows, LANES))
    edge_planes = 3 + fractions + 2 + 6
    side, bed, code, send_a, send_b, framed = pl.pallas_call(
        functools.partial(mid_kernel, (band_cols, cols_count, strip_rows, narrow)),
        out_shape=(
            f32((6, tile_rows, LANES)), f32((tile_rows, LANES)), jax.ShapeDtypeStruct((tile_rows, LANES), jnp.int32),
            f32((edge_planes, SUB, LANES)), f32((edge_planes, SUB, LANES)), f32((band_rows + 2 * SUB, LANES)),
        ),
        in_specs=[vmem()] * 7 + [smem()], out_specs=(vmem(),) * 6,
    )(water_depth, discharge, sediment, wet_mask, cell_map, packs, frame, place)

    pairs_a = [p for i in range(0, rows_count - 1, 2) for p in ((i, i + 1), (i + 1, i))]
    pairs_b = [p for i in range(1, rows_count - 1, 2) for p in ((i, i + 1), (i + 1, i))]
    recv_a = lax.ppermute(send_a, "row", pairs_a)
    recv_b = lax.ppermute(send_b, "row", pairs_b)

    channels = 3 + fractions
    span = tile_rows + 2 * RIM + 2 * SUB
    space = functools.partial(pltpu.VMEM, dtype=jnp.float32)
    depth_out, discharge_out, sediment_out, partial = pl.pallas_call(
        flow_kernel,
        out_shape=(
            f32(water_depth.shape), f32(discharge.shape), f32(sediment.shape), f32((fractions * band_rows, LANES)),
        ),
        in_specs=[vmem()] * 7 + [smem()] * 2 + [vmem()] * 2, out_specs=(vmem(),) * 4,
        scratch_shapes=[
            space((2, channels, span, LANES)), space((2, 4, span, LANES)), space((7, span, LANES)),
            space((7, span, LANES)), space((channels, span, LANES)), space((4, span, LANES)),
            space((channels, span, LANES)), space((4, span, LANES)), space((fractions, span, LANES)),
            pltpu.VMEM((tile_rows, LANES), jnp.int32),
        ],
    )(water_depth, discharge, sediment, wet_mask, bed, side, code, sediment_params, place, recv_a, recv_b)

    sums = lax.all_gather(partial, "col", axis=0)
    geometry = (band_cols if narrow else LANES, cols_count, strip_rows)
    if narrow:
        look_cells = cell_map
    else:
        wide = jnp.zeros((fractions, band_rows, band_cols + 2 * LANES), jnp.float32)
        for d in range(cols_count):
            start = LANES + d * (tile_cols // 4) - (LANES - tile_cols // 4) // 2
            wide = wide.at[:, :, start : start + LANES].add(sums[d].reshape(fractions, band_rows, LANES))
        share = lax.dynamic_slice_in_dim(wide, col_at * strip_rows, strip_rows, axis=1)[:, :, LANES:-LANES]
        deposit_wide = exner_factor / 16.0 * share
        bed_wide = bed_level + jnp.sum(deposit_wide, axis=0)
        sums = lax.dynamic_slice_in_dim(wide, frame_start + LANES, LANES, axis=2).reshape(1, -1, LANES)
        geometry = (LANES, 1, strip_rows)
        look_cells = cell_map // band_cols * LANES + cell_map % band_cols - frame_start
    bed_new, deposit, fine_bed = pl.pallas_call(
        functools.partial(bed_kernel, geometry),
        out_shape=(f32((strip_rows, LANES)), f32((fractions, strip_rows, LANES)), f32((tile_rows, LANES))),
        in_specs=[vmem()] * 3 + [smem()], out_specs=(vmem(),) * 3,
        scratch_shapes=[space((band_rows + 2 * SUB, LANES)), space((fractions * band_rows, LANES))],
    )(sums, framed, look_cells, place)
    if not narrow:
        bed_new, deposit = bed_wide, deposit_wide
    return (depth_out, discharge_out, sediment_out, fine_bed, bed_new, deposit)


def solution(mesh):
    placed = (
        P("row", "col"),
        P(None, "row", "col"),
        P(None, "row", "col"),
        P(("row", "col"), None),
        P("row", "col"),
        P("row", "col"),
        P(),
    )
    return jax.shard_map(
        local,
        mesh=mesh,
        in_specs=placed,
        out_specs=(
            P("row", "col"),
            P(None, "row", "col"),
            P(None, "row", "col"),
            P("row", "col"),
            P(("row", "col"), None),
            P(None, ("row", "col"), None),
        ),
        check_vma=False,
    )
```

profile of v0, /device:TPU:25, one launch (start us, length us, event | category | flops | bytes accessed | tf_op | source)
XLA Modules:
  0.0 46.8 jit_solution(16860537005027005829)
XLA Ops:
  0.6 1.8 %shard_map.118 = f32[136,128]{1,0:T(8,128)} custom-call(f32[64,128]{1,0:T(8,128)} %depth.5, f32[2,64,128]{2,1,0:T(8,128)} %flow.5, f32[4,64,128]{2,1,0:T(8,128)} %mud.5, s32[64,128]{1,0:T(8,128)} %wet.5, s32[64,128]{1,0:T(8,128)} %cells.5, f32[4,128]{1,0:T(4,128)} %strip.1), custom_call_target="tpu_custom_call" | custom-call | tf_op jit(solution)/shard_map/pallas_call | solution.py:465
  2.5 7.9 %all-gather = f32[544,128]{1,0:T(8,128)} all-gather(f32[136,128]{1,0:T(8,128)} %shard_map.118), channel_id=2, replica_groups=mesh['row'=8,'col'=4] {'col'}, dimensions={0}, use_global_device_ids=true | all-gather | bytes 348160 | tf_op jit(solution)/shard_map/all_gather | solution.py:468
  10.4 0.6 %pad_add_fusion.place = s32[4]{0:T(128)} fusion(s32[1]{0:T(128)} %bitcast.3, s32[1]{0:T(128)} %constant.13.clone.1, s32[1]{0:T(128)} %bitcast.2, s32[1]{0:T(128)} %bitcast.1), kind=kLoop, calls=%fused_computation | loop fusion | flops 12 | bytes 32 | tf_op jit(solution)/shard_map/stack | solution.py:461
  11.0 0.6 %broadcast_in_dim.3.frame = f32[8,128]{1,0:T(8,128)} broadcast(f32[]{:T(128)} %constant.3.clone.1), dimensions={} | broadcast | bytes 4100 | tf_op jit(solution)/shard_map/broadcast_in_dim | solution.py:471
  11.6 2.9 %shard_map.119 = (f32[6,64,128]{2,1,0:T(8,128)}, f32[64,128]{1,0:T(8,128)}, s32[64,128]{1,0:T(8,128)}, f32[15,8,128]{2,1,0:T(8,128)}, f32[15,8,128]{2,1,0:T(8,128)}, /*index=5*/f32[32,128]{1,0:T(8,128)}) custom-call(f32[64,128]{1,0:T(8,128)} %depth.5, f32[2,64,128]{2,1,0:T(8,128)} %flow.5, f32[4,64,128]{2,1,0:T(8,128)} %mud.5, s32[64,128]{1,0:T(8,128)} %wet.5, ...), custom_call_target="tpu_custom_call" | custom-call | tf_op jit(solution)/shard_map/pallas_call | solution.py:478
  14.5 1.2 %collective-permute-start = (f32[15,8,128]{2,1,0:T(8,128)}, f32[15,8,128]{2,1,0:T(8,128)S(1)}, u32[]{:S(2)}, u32[]{:S(2)}) collective-permute-start(f32[15,8,128]{2,1,0:T(8,128)} %get-tuple-element.22), channel_id=1, source_target_pairs={{0,4},{4,0},{8,12},{12,8},{16,20},{20,16},{24,28},{28,24},{1,5},{5... | collective-permute-start | bytes 184328 | tf_op jit(solution)/shard_map/ppermute | solution.py:489
  15.7 2.0 %collective-permute-start.1 = (f32[15,8,128]{2,1,0:T(8,128)}, f32[15,8,128]{2,1,0:T(8,128)S(1)}, u32[]{:S(2)}, u32[]{:S(2)}) collective-permute-start(f32[15,8,128]{2,1,0:T(8,128)} %get-tuple-element.23), channel_id=1, source_target_pairs={{4,8},{8,4},{12,16},{16,12},{20,24},{24,20},{5,9},{9,5},{13,17},{1... | collective-permute-start | bytes 184328 | tf_op jit(solution)/shard_map/ppermute | solution.py:490
  17.7 0.4 collective-permute-done.recv_a
  18.1 0.0 copy-start
  18.1 3.7 %collective-permute-done.1.recv_b = f32[15,8,128]{2,1,0:T(8,128)S(1)} collective-permute-done((f32[15,8,128]{2,1,0:T(8,128)}, f32[15,8,128]{2,1,0:T(8,128)S(1)}, u32[]{:S(2)}, u32[]{:S(2)}) %collective-permute-start.1) | collective-permute-done | bytes 61472 | tf_op jit(solution)/shard_map/ppermute | solution.py:490
  21.8 0.0 copy-start.1
  21.8 0.0 copy-done
  21.8 0.6 %copy-done.1 = f32[15,8,128]{2,1,0:T(8,128)} copy-done((f32[15,8,128]{2,1,0:T(8,128)}, f32[15,8,128]{2,1,0:T(8,128)S(1)}, u32[]{:S(2)}) %copy-start.1) | copy-done | bytes 61464
  22.4 15.2 %shard_map.120 = (f32[64,128]{1,0:T(8,128)}, f32[2,64,128]{2,1,0:T(8,128)}, f32[4,64,128]{2,1,0:T(8,128)}, f32[64,128]{1,0:T(8,128)}) custom-call(f32[64,128]{1,0:T(8,128)} %depth.5, f32[2,64,128]{2,1,0:T(8,128)} %flow.5, f32[4,64,128]{2,1,0:T(8,128)} %mud.5, s32[64,128]{1,0:T(8,128)} %wet.5, f32[64,128]{1,0:T(8,128)} %get-tuple-element.19.bed, ...), custom_call_target="tpu_custom_call" | custom-call | tf_op jit(solution)/shard_map/pallas_call | solution.py:495
  37.6 7.5 %all-gather.1 = f32[256,128]{1,0:T(8,128)} all-gather(f32[64,128]{1,0:T(8,128)} %get-tuple-element.27), channel_id=3, replica_groups=mesh['row'=8,'col'=4] {'col'}, dimensions={0}, use_global_device_ids=true | all-gather | bytes 163840 | tf_op jit(solution)/shard_map/all_gather | solution.py:509
  45.1 1.7 %shard_map.121 = (f32[4,128]{1,0:T(4,128)}, f32[4,4,128]{2,1,0:T(4,128)}, f32[64,128]{1,0:T(8,128)}) custom-call(f32[4,64,128]{2,1,0:T(8,128)} %bitcast.6, f32[32,128]{1,0:T(8,128)} %get-tuple-element.28.bed, s32[64,128]{1,0:T(8,128)} %cells.5, s32[4]{0:T(128)} %pad_add_fusion.place), custom_call_target="tpu_custom_call" | custom-call | tf_op jit(solution)/shard_map/pallas_call | solution.py:524
Async XLA Ops:
  14.5 3.6 %collective-permute-start = (f32[15,8,128]{2,1,0:T(8,128)}, f32[15,8,128]{2,1,0:T(8,128)S(1)}, u32[]{:S(2)}, u32[]{:S(2)}) collective-permute-start(f32[15,8,128]{2,1,0:T(8,128)} %get-tuple-element.22), channel_id=1, source_target_pairs={{0,4},{4,0},{8,12},{12,8},{16,20},{20,16},{24,28},{28,24},{1,5},{5... | collective-permute-start | bytes 184328 | tf_op jit(solution)/shard_map/ppermute | solution.py:489
  15.7 6.1 %collective-permute-start.1 = (f32[15,8,128]{2,1,0:T(8,128)}, f32[15,8,128]{2,1,0:T(8,128)S(1)}, u32[]{:S(2)}, u32[]{:S(2)}) collective-permute-start(f32[15,8,128]{2,1,0:T(8,128)} %get-tuple-element.23), channel_id=1, source_target_pairs={{4,8},{8,4},{12,16},{16,12},{20,24},{24,20},{5,9},{9,5},{13,17},{1... | collective-permute-start | bytes 184328 | tf_op jit(solution)/shard_map/ppermute | solution.py:490
  18.1 3.7 %copy-start = (f32[15,8,128]{2,1,0:T(8,128)}, f32[15,8,128]{2,1,0:T(8,128)S(1)}, u32[]{:S(2)}) copy-start(f32[15,8,128]{2,1,0:T(8,128)S(1)} %collective-permute-done.recv_a) | copy-start | bytes 184324
  21.8 0.6 %copy-start.1 = (f32[15,8,128]{2,1,0:T(8,128)}, f32[15,8,128]{2,1,0:T(8,128)S(1)}, u32[]{:S(2)}) copy-start(f32[15,8,128]{2,1,0:T(8,128)S(1)} %collective-permute-done.1.recv_b) | copy-start | bytes 184324
where the time goes:
time: 47.1 us; the launch traced here: 46.8 us
  Pallas kernels  21.6 us (46%)
  blocking collectives  15.4 us (33%)
  waiting for transfers between devices  4.04 us (9%)
  starting transfers between devices  3.25 us (7%)
  local copies, waits for them, and re-layouts  1.22 us (3%)
  between operations  0.65 us (1%)
  other arithmetic  0.58 us (1%)
    pallas_call x1, Pallas kernels, local(): pl.pallas_call(flow_kernel, out_shape=(f32(water_depth.shape), f32(discha...  15.2 us
    all_gather x1, blocking collectives, local(): packs = lax.all_gather(packed, 'col', axis=0)  7.94 us
    all_gather x1, blocking collectives, local(): sums = lax.all_gather(partial, 'col', axis=0)  7.49 us
    ppermute x1, waiting for transfers between devices, local(): recv_b = lax.ppermute(send_b, 'row', pairs_b)  3.69 us
    pallas_call x1, Pallas kernels, local(): pl.pallas_call(functools.partial(mid_kernel, (band_cols, cols_count, stri...  2.91 us
    ppermute x1, starting transfers between devices, local(): recv_b = lax.ppermute(send_b, 'row', pairs_b)  2.01 us
    pallas_call x1, Pallas kernels, local(): pl.pallas_call(pack_kernel, out_shape=f32((pack_rows, LANES)), in_specs=[...  1.83 us
    pallas_call x1, Pallas kernels, local(): pl.pallas_call(functools.partial(bed_kernel, geometry), out_shape=(f32((s...  1.69 us
  transfers between devices with their start and end apart: 2, of which 2 were waited for; matrix products, arithmetic and copies ran while one was open for 0% of the time, Pallas kernels for 0%

commit v1 on v0

--- a/solution.py
+++ b/solution.py
@@ -10,6 +10,7 @@
 SUBSTEPS = 4
 LANES = 128
 SUB = 8
+UNROLL = 2
 RIM = 2 * SUBSTEPS
 
 gravity = 1.0
@@ -34,6 +35,10 @@
     return lax.broadcasted_iota(jnp.int32, shape, len(shape) - 1)
 
 
+def params_of(limit=16 << 20):
+    return pltpu.CompilerParams(vmem_limit_bytes=limit)
+
+
 def pick(table, index):
     return jnp.take_along_axis(table, index, axis=1, mode="promise_in_bounds")
 
@@ -47,25 +52,39 @@
     return out
 
 
+def folded_rows(rows):
+    return -(-rows // SUB // (LANES // (2 * RIM)))
+
+
 def pack_kernel(depth, flow, mud, wet, cells, strip, out):
     rows = depth.shape[0]
     planes = planes_of(depth, flow, mud, wet, cells)
     group = lane_ids((SUB, LANES)) // RIM
-    for start in range(0, rows, SUB):
-        at = pl.ds(start, SUB)
-        low = jnp.zeros((SUB, LANES), jnp.float32)
-        high = low
+    pairs = LANES // (2 * RIM)
+    spare = [[None] * folded_rows(rows) for _ in planes[pairs:]]
+    for block in range(rows // SUB):
+        at = pl.ds(block * SUB, SUB)
+        packed = None
         for p, plane in enumerate(planes):
             x = plane(at)
-            low = jnp.where(group == p, pltpu.roll(x, RIM * p, 1) if p else x, low)
-            high = jnp.where(group == p, pltpu.roll(x, (RIM * p + RIM) % LANES, 1), high)
-        out[at, :] = low
-        out[pl.ds(rows + start, SUB), :] = high
+            slot = p if p < pairs else block % pairs
+            low = pltpu.roll(x, 2 * RIM * slot, 1) if slot else x
+            high = pltpu.roll(x, (2 * RIM * slot + 2 * RIM) % LANES, 1)
+            old = packed if p < pairs else spare[p - pairs][block // pairs]
+            both = jnp.where(group == 2 * slot, low, high)
+            new = both if old is None else jnp.where(group // 2 == slot, both, old)
+            if p < pairs:
+                packed = new
+            else:
+                spare[p - pairs][block // pairs] = new
+        out[at, :] = packed
+    start = rows
+    for x in [x for p in spare for x in p]:
+        out[pl.ds(start, SUB), :] = x
+        start += SUB
     strip_rows = strip.shape[0]
     for chunk in range(strip.shape[1] // LANES):
-        out[pl.ds(2 * rows + chunk * strip_rows, strip_rows), :] = strip[
-            :, chunk * LANES : (chunk + 1) * LANES
-        ]
+        out[pl.ds(start + chunk * strip_rows, strip_rows), :] = strip[:, chunk * LANES : (chunk + 1) * LANES]
 
 
 def spread_rows(frame_ref, block, shift):
@@ -93,66 +112,84 @@
     return jnp.where(shift == 0, found, jnp.where(shift < 0, below, above))
 
 
-def fill_frame(frame_ref, band_rows, rows_of):
+def starts_of(col_at, band_cols):
+    coarse_start = col_at * (LANES // 4)
+    return coarse_start, 0 if band_cols == LANES else coarse_start - (LANES - LANES // 4) // 2
+
+
+def fill_frame(frame_ref, rows_of):
     frame_ref[...] = jnp.zeros_like(frame_ref)
     for r0, value in rows_of:
         frame_ref[pl.ds(SUB + r0, value.shape[0]), :] = value
 
 
 def mid_kernel(
-    geometry, depth, flow, mud, wet, cells, packs, frame, place,
-    side, bed, code, send_a, send_b, frame_ref,
+    geometry, depth, flow, mud, wet, cells, packs, *refs
 ):
+    band_cols, cols_count, strip_rows, from_packs = geometry
+    frame = None if from_packs else refs[0]
+    side, bed, code, send_a, send_b, frame_ref = refs[0 if from_packs else 1 :]
     rows = depth.shape[0]
     fractions = mud.shape[0]
-    band_cols, cols_count, strip_rows, from_packs = geometry
-    row_at, col_at, frame_start = place[0], place[1], place[2]
-    coarse_start = place[3]
+    row_at, col_at = lax.axis_index("row"), lax.axis_index("col")
+    coarse_start, frame_start = starts_of(col_at, band_cols)
+    planes = planes_of(depth, flow, mud, wet, cells)
+    count = len(planes)
+    wet_at, cell_at = count - 2, count - 1
+    pairs = LANES // (2 * RIM)
+    strip_at = rows + (count - pairs) * folded_rows(rows) * SUB
     if from_packs:
         fill_frame(
-            frame_ref, None,
-            [(d * strip_rows, packs[d, pl.ds(2 * rows, strip_rows), :]) for d in range(cols_count)],
+            frame_ref,
+            [(d * strip_rows, packs[d, pl.ds(strip_at, strip_rows), :]) for d in range(cols_count)],
         )
     else:
-        fill_frame(frame_ref, None, [(0, frame[...])])
+        fill_frame(frame_ref, [(0, frame[...])])
     lane = lane_ids((SUB, LANES))
     width = 4 * RIM
     inside = lane % width
     group = lane // width
     is_low = inside < RIM
     is_high = inside >= 3 * RIM
-    own_index = jnp.where(
-        is_low | is_high, 0, jnp.where(inside < 2 * RIM, inside - RIM, inside - 2 * RIM + LANES - RIM)
-    )
+    is_first = inside < 2 * RIM
     has_low = jnp.where(col_at > 0, 1.0, 0.0)
     has_high = jnp.where(col_at < cols_count - 1, 1.0, 0.0)
     scale = jnp.where(is_low, has_low, jnp.where(is_high, has_high, 1.0))
     left = jnp.maximum(col_at - 1, 0)
     right = jnp.minimum(col_at + 1, cols_count - 1)
-    planes = planes_of(depth, flow, mud, wet, cells)
-    count = len(planes)
-    wet_at, cell_at = count - 2, count - 1
     parity = row_at % 2
+
+    def turn(x, shift):
+        shift = shift % LANES
+        return pltpu.roll(x, shift, 1) if shift else x
+
     for block in range(rows // SUB):
         at = pl.ds(block * SUB, SUB)
-        from_left = packs[left, pl.ds(rows + block * SUB, SUB), :]
-        from_right = packs[right, pl.ds(block * SUB, SUB), :]
-
-        def side_of(own, p):
-            index = p * RIM + lane % RIM
-            x = jnp.where(is_low, pick(from_left, index), jnp.where(is_high, pick(from_right, index), own))
-            return x * scale
-
-        def own_of(p):
-            return pick(planes[p](at), own_index)
-
-        sides = [side_of(own_of(p), p) for p in range(3)]
-        own = own_of(3)
+
+        def gather_to(p, base):
+            if p < pairs:
+                source, slot = at, p
+            else:
+                source = pl.ds(rows + ((p - pairs) * folded_rows(rows) + block // pairs) * SUB, SUB)
+                slot = block % pairs
+            x = planes[p](at)
+            low = turn(packs[left, source, :], base - 2 * RIM * slot - RIM)
+            high = turn(packs[right, source, :], base + 3 * RIM - 2 * RIM * slot)
+            own = jnp.where(is_first, turn(x, base + RIM), turn(x, base + 3 * RIM))
+            return jnp.where(is_low, low, jnp.where(is_high, high, own))
+
+        def for_all(p):
+            x = gather_to(p, 0)
+            x = jnp.where(lane < width, x, pltpu.roll(x, width, 1))
+            return jnp.where(lane < 2 * width, x, pltpu.roll(x, 2 * width, 1)) * scale
+
+        sides = [for_all(p) for p in range(3)]
+        each = gather_to(3, 0)
         for k in range(1, fractions):
-            own = jnp.where(group == k, own_of(3 + k), own)
-        sides.append(side_of(own, 3 + group))
-        sides.append(side_of(own_of(wet_at), wet_at))
-        side_row, side_col = split_cells(side_of(own_of(cell_at), cell_at), band_cols)
+            each = jnp.where(group == k, gather_to(3 + k, k * width), each)
+        sides.append(each * scale)
+        sides.append(for_all(wet_at))
+        side_row, side_col = split_cells(for_all(cell_at), band_cols)
         side_at = jnp.where(scale > 0.0, side_col - frame_start, 0)
         sides.append(lookup(frame_ref, block, row_shift_of(side_row, block), side_at) * scale)
         cell_row, cell_col = split_cells(cells[at, :].astype(jnp.float32), band_cols)
@@ -196,7 +233,7 @@
 
 
 def flow_kernel(
-    depth, flow, mud, wet, bed, side, code, params, place, recv_a, recv_b,
+    band_cols, depth, flow, mud, wet, bed, side, code, params, recv_a, recv_b,
     depth_out, flow_out, mud_out, partial,
     q_main, q_side, static_main, static_side, slope_main, slope_side, flux_main, flux_side, exchanged, code_ref,
 ):
@@ -206,7 +243,7 @@
     top = SUB
     body = top + RIM
     blocks = (rows + 2 * RIM) // SUB
-    parity = place[0] % 2
+    parity = lax.axis_index("row") % 2
     lane = lane_ids((SUB, LANES))
     width = 4 * RIM
     group = lane // width
@@ -242,16 +279,19 @@
     side_coeffs = ([by_group(settle[0])], [by_group(inv_crit[0])], [by_group(erode[0])])
     main_coeffs = (settle[0], inv_crit[0], erode[0])
 
-    def edge_fix(k):
-        g = (k - 3) if k >= 3 else 0
-        return jnp.where(lane == 0, g * width + RIM - 1, jnp.where(lane == LANES - 1, g * width + 3 * RIM, 0))
-
-    def flux_fix(k):
-        g = (k - 3) if k >= 3 else 0
-        return jnp.where(lane == 0, g * width + RIM - 1, jnp.where(lane == LANES - 1, g * width + 3 * RIM - 1, 0))
-
-    edge_index = [edge_fix(max(k, 3)) for k in range(3, 3 + fractions)]
-    flux_index = [flux_fix(max(k, 3)) for k in range(3, 3 + fractions)]
+    def turn(x, shift):
+        shift = shift % LANES
+        return pltpu.roll(x, shift, 1) if shift else x
+
+    def start_of(k):
+        return max(k - 3, 0) * width
+
+    def low_edge(x, k):
+        return turn(x, 1 - RIM - start_of(k))
+
+    def high_edge(x, k):
+        return turn(x, LANES - 1 - 3 * RIM - start_of(k))
+
     first_lane = lane == 0
     last_lane = lane == LANES - 1
 
@@ -268,11 +308,10 @@
             w_right, b_right = pltpu.roll(w, LANES - 1, 1), pltpu.roll(b, LANES - 1, 1)
             b_left = pltpu.roll(b, 1, 1)
             if is_main:
-                w_edge = pick(rows_at(static_side, wet_main, r0), edge_index[0])
-                b_edge = pick(rows_at(static_side, bed_main, r0), edge_index[0])
-                w_right = jnp.where(last_lane, w_edge, w_right)
-                b_right = jnp.where(last_lane, b_edge, b_right)
-                b_left = jnp.where(first_lane, b_edge, b_left)
+                w_edge, b_edge = rows_at(static_side, wet_main, r0), rows_at(static_side, bed_main, r0)
+                w_right = jnp.where(last_lane, high_edge(w_edge, 0), w_right)
+                b_right = jnp.where(last_lane, high_edge(b_edge, 0), b_right)
+                b_left = jnp.where(first_lane, low_edge(b_edge, 0), b_left)
             at = pl.ds(r0, SUB)
             ref[2, at, :] = 0.5 * (w * rows_at(ref, wet_main, r0 + 1))
             ref[3, at, :] = 0.5 * (w * w_right)
@@ -306,9 +345,8 @@
         for k in range(n):
             before, after = pltpu.roll(here[k], 1, 1), pltpu.roll(here[k], LANES - 1, 1)
             if edges is not None:
-                edge = pick(edges[min(k, 3)], edge_index[max(k - 3, 0)])
-                before = jnp.where(first_lane, edge, before)
-                after = jnp.where(last_lane, edge, after)
+                before = jnp.where(first_lane, low_edge(edges[min(k, 3)], k), before)
+                after = jnp.where(last_lane, high_edge(edges[min(k, 3)], k), after)
             s = half_minmod(before, here[k], after)
             lefts.append(here[k] + s)
             rights.append(pltpu.roll(here[k] - s, LANES - 1, 1))
@@ -340,6 +378,7 @@
         at = pl.ds(r0, SUB)
         last = level == SUBSTEPS - 1
         qs, qm = q_side.at[level % 2], q_main.at[level % 2]
+        slopes(block + 1, level)
         if rows_only:
             row_fluxes(qm, slope_main, flux_main, static_main, channels, r0)
             return
@@ -355,9 +394,9 @@
         here = [rows_at(qm, k, r0) for k in range(channels)]
         fluxes = col_fluxes(here, static_main, channels, r0, edges)
         for k in range(channels):
-            edge = pick(side_flux[min(k, 3)], flux_index[max(k - 3, 0)])
-            f = jnp.where(last_lane, edge, fluxes[k])
-            net[k] = net[k] + (jnp.where(first_lane, edge, pltpu.roll(fluxes[k], 1, 1)) - f)
+            edge = side_flux[min(k, 3)]
+            f = jnp.where(last_lane, turn(edge, LANES - 3 * RIM - start_of(k)), fluxes[k])
+            net[k] = net[k] + (jnp.where(first_lane, low_edge(edge, k), pltpu.roll(fluxes[k], 1, 1)) - f)
         new, changes = update(here, net, static_main, main_coeffs, r0)
         if last:
             out = pl.ds(pl.multiple_of(r0 - body, SUB), SUB)
@@ -378,20 +417,16 @@
     for level in range(SUBSTEPS):
         last = level == SUBSTEPS - 1
 
-        def slope_step(block, carry, level=level):
-            slopes(block, level)
-            return carry
-
         def advance_step(block, carry, level=level):
             advance(block, level)
             return carry
 
-        lax.fori_loop(0, blocks, slope_step, 0)
+        slopes(0, level)
         if last:
             advance(0, level, rows_only=True)
-            lax.fori_loop(1, blocks - 1, advance_step, 0)
+            lax.fori_loop(1, blocks - 1, advance_step, 0, unroll=UNROLL)
         else:
-            lax.fori_loop(0, blocks, advance_step, 0)
+            lax.fori_loop(0, blocks, advance_step, 0, unroll=UNROLL)
 
     coarse_rows = rows // 4
     code_ref[...] = code[...]
@@ -399,7 +434,8 @@
     codes = [code_ref[pl.ds(k, coarse_rows, stride=4), :] for k in range(4)]
     to_coarse = (
         lax.broadcasted_iota(jnp.int32, (LANES, LANES), 0) // 4 == lax.broadcasted_iota(jnp.int32, (LANES, LANES), 1)
-    ).astype(jnp.float32)
+    ).astype(jnp.bfloat16)
+    coarse_start, frame_start = starts_of(lax.axis_index("col"), band_cols)
     total = None
     for col_shift in range(7):
         sums = [None] * fractions
@@ -413,16 +449,19 @@
                 if row_shift != 1:
                     part = pltpu.roll(part, 1 if row_shift == 2 else coarse_rows - 1, 0)
                 sums[f] = part if sums[f] is None else sums[f] + part
-        z = jnp.dot(
-            jnp.concatenate(sums, axis=0), to_coarse, precision=lax.Precision.HIGHEST,
-            preferred_element_type=jnp.float32,
-        )
-        z = pltpu.roll(z, (place[3] - place[2] + col_shift - 3 + LANES) % LANES, 1)
+        rest = jnp.concatenate(sums, axis=0)
+        z = None
+        for _ in range(3):
+            term = rest.astype(jnp.bfloat16)
+            rest = rest - term.astype(jnp.float32)
+            moved = jnp.dot(term, to_coarse, preferred_element_type=jnp.float32)
+            z = moved if z is None else z + moved
+        z = pltpu.roll(z, (coarse_start - frame_start + col_shift - 3 + LANES) % LANES, 1)
         total = z if total is None else total + z
     partial[...] = total
 
 
-def bed_kernel(geometry, sums, bed, cells, place, bed_out, deposit_out, fine, frame_ref, total_ref):
+def bed_kernel(geometry, sums, bed, cells, bed_out, deposit_out, fine, frame_ref, total_ref):
     band_cols, cols_count, strip_rows = geometry
     rows = cells.shape[0]
     band_rows = rows // 4
@@ -431,7 +470,7 @@
     for d in range(1, cols_count):
         total = total + sums[d]
     total_ref[...] = (exner_factor / 16.0) * total
-    at = place[1] * strip_rows
+    at = lax.axis_index("col") * strip_rows
     frame_ref[...] = jnp.zeros_like(frame_ref)
     whole = None
     for f in range(fractions):
@@ -454,26 +493,25 @@
     rows_count = lax.axis_size("row")
     band_rows = tile_rows // 4
     f32 = functools.partial(jax.ShapeDtypeStruct, dtype=jnp.float32)
-    row_at, col_at = lax.axis_index("row"), lax.axis_index("col")
-    coarse_start = col_at * (tile_cols // 4)
     narrow = band_cols == LANES
-    frame_start = 0 * coarse_start if narrow else coarse_start - (LANES - tile_cols // 4) // 2
-    place = jnp.stack([row_at, col_at, frame_start, coarse_start]).astype(jnp.int32)
+    col_at = lax.axis_index("col")
+    frame_start = starts_of(col_at, band_cols)[1]
     chunks = band_cols // LANES
-    pack_rows = 2 * tile_rows + -(-chunks * strip_rows // SUB) * SUB
+    extra = (5 + fractions - LANES // (2 * RIM)) * folded_rows(tile_rows) * SUB
+    pack_rows = tile_rows + extra + -(-chunks * strip_rows // SUB) * SUB
 
     packed = pl.pallas_call(
         pack_kernel, out_shape=f32((pack_rows, LANES)), in_specs=[vmem()] * 6, out_specs=vmem(),
+        compiler_params=params_of(),
     )(water_depth, discharge, sediment, wet_mask, cell_map, bed_level)
     packs = lax.all_gather(packed, "col", axis=0)
 
-    if narrow:
-        frame = jnp.zeros((SUB, LANES), jnp.float32)
-    else:
-        strips = packs[:, 2 * tile_rows : 2 * tile_rows + chunks * strip_rows]
+    frames = []
+    if not narrow:
+        strips = packs[:, tile_rows + extra : tile_rows + extra + chunks * strip_rows]
         band = strips.reshape(cols_count, chunks, strip_rows, LANES).transpose(0, 2, 1, 3).reshape(band_rows, band_cols)
         wide = jnp.pad(band, ((0, 0), (LANES, LANES)))
-        frame = lax.dynamic_slice(wide, (jnp.int32(0), frame_start + LANES), (band_rows, LANES))
+        frames = [lax.dynamic_slice(wide, (jnp.int32(0), frame_start + LANES), (band_rows, LANES))]
     edge_planes = 3 + fractions + 2 + 6
     side, bed, code, send_a, send_b, framed = pl.pallas_call(
         functools.partial(mid_kernel, (band_cols, cols_count, strip_rows, narrow)),
@@ -481,8 +519,8 @@
             f32((6, tile_rows, LANES)), f32((tile_rows, LANES)), jax.ShapeDtypeStruct((tile_rows, LANES), jnp.int32),
             f32((edge_planes, SUB, LANES)), f32((edge_planes, SUB, LANES)), f32((band_rows + 2 * SUB, LANES)),
         ),
-        in_specs=[vmem()] * 7 + [smem()], out_specs=(vmem(),) * 6,
-    )(water_depth, discharge, sediment, wet_mask, cell_map, packs, frame, place)
+        in_specs=[vmem()] * (6 + len(frames)), out_specs=(vmem(),) * 6, compiler_params=params_of(),
+    )(water_depth, discharge, sediment, wet_mask, cell_map, packs, *frames)
 
     pairs_a = [p for i in range(0, rows_count - 1, 2) for p in ((i, i + 1), (i + 1, i))]
     pairs_b = [p for i in range(1, rows_count - 1, 2) for p in ((i, i + 1), (i + 1, i))]
@@ -490,21 +528,21 @@
     recv_b = lax.ppermute(send_b, "row", pairs_b)
 
     channels = 3 + fractions
-    span = tile_rows + 2 * RIM + 2 * SUB
+    span = tile_rows + 2 * RIM + 3 * SUB
     space = functools.partial(pltpu.VMEM, dtype=jnp.float32)
     depth_out, discharge_out, sediment_out, partial = pl.pallas_call(
-        flow_kernel,
+        functools.partial(flow_kernel, band_cols),
         out_shape=(
             f32(water_depth.shape), f32(discharge.shape), f32(sediment.shape), f32((fractions * band_rows, LANES)),
         ),
-        in_specs=[vmem()] * 7 + [smem()] * 2 + [vmem()] * 2, out_specs=(vmem(),) * 4,
+        in_specs=[vmem()] * 7 + [smem()] + [vmem()] * 2, out_specs=(vmem(),) * 4, compiler_params=params_of(),
         scratch_shapes=[
             space((2, channels, span, LANES)), space((2, 4, span, LANES)), space((7, span, LANES)),
             space((7, span, LANES)), space((channels, span, LANES)), space((4, span, LANES)),
             space((channels, span, LANES)), space((4, span, LANES)), space((fractions, span, LANES)),
             pltpu.VMEM((tile_rows, LANES), jnp.int32),
         ],
-    )(water_depth, discharge, sediment, wet_mask, bed, side, code, sediment_params, place, recv_a, recv_b)
+    )(water_depth, discharge, sediment, wet_mask, bed, side, code, sediment_params, recv_a, recv_b)
 
     sums = lax.all_gather(partial, "col", axis=0)
     geometry = (band_cols if narrow else LANES, cols_count, strip_rows)
@@ -524,9 +562,9 @@
     bed_new, deposit, fine_bed = pl.pallas_call(
         functools.partial(bed_kernel, geometry),
         out_shape=(f32((strip_rows, LANES)), f32((fractions, strip_rows, LANES)), f32((tile_rows, LANES))),
-        in_specs=[vmem()] * 3 + [smem()], out_specs=(vmem(),) * 3,
+        in_specs=[vmem()] * 3, out_specs=(vmem(),) * 3, compiler_params=params_of(),
         scratch_shapes=[space((band_rows + 2 * SUB, LANES)), space((fractions * band_rows, LANES))],
-    )(sums, framed, look_cells, place)
+    )(sums, framed, look_cells)
     if not narrow:
         bed_new, deposit = bed_wide, deposit_wide
     return (depth_out, discharge_out, sediment_out, fine_bed, bed_new, deposit)

time: 47.1 us -> 39.5 us (0.84)
  Pallas kernels: 21.6 us -> 12.8 us
  local copies, waits for them, and re-layouts: 1.22 us -> 5.37 us
  blocking collectives: 15.4 us -> 13 us
  other arithmetic: 0.58 us -> 0 us
    pallas_call x1, Pallas kernels: 15.2 us -> 9.2 us  [local(): pl.pallas_call(functools.partial(flow_kernel, band_cols), out_shape=(f32(...]
    unnamed x4 -> x16, local copies, waits for them, and re-layouts: 0.63 us -> 5.37 us
    all_gather x1, blocking collectives: 7.94 us -> 6.02 us  [local(): packs = lax.all_gather(packed, 'col', axis=0)]
    pallas_call x1, Pallas kernels: 1.83 us -> 0.2 us  [local(): pl.pallas_call(pack_kernel, out_shape=f32((pack_rows, LANES)), in_specs=[...]
    pallas_call x1, Pallas kernels: 1.69 us -> 0.75 us  [local(): pl.pallas_call(functools.partial(bed_kernel, geometry), out_shape=(f32((s...]
    broadcast_in_dim x1 -> x0, local copies, waits for them, and re-layouts: 0.59 us -> none  [local(): frame = jnp.zeros((SUB, LANES), jnp.float32)]
    another operation x1 -> x0, other arithmetic: 0.58 us -> none  [local(): jnp.stack([row_at, col_at, frame_start, coarse_start]).astype(jnp.int32)]
    all_gather x1, blocking collectives: 7.49 us -> 6.96 us  [local(): sums = lax.all_gather(partial, 'col', axis=0)]
where the time goes in v1:
time: 39.5 us; the launch traced here: 39 us
  blocking collectives  13 us (33%)
  Pallas kernels  12.8 us (32%)
  local copies, waits for them, and re-layouts  5.37 us (14%)
  waiting for transfers between devices  3.83 us (10%)
  starting transfers between devices  3.31 us (8%)
  between operations  0.67 us (2%)
    pallas_call x1, Pallas kernels, local(): pl.pallas_call(functools.partial(flow_kernel, band_cols), out_shape=(f32(...  9.2 us
    all_gather x1, blocking collectives, local(): sums = lax.all_gather(partial, 'col', axis=0)  6.96 us
    all_gather x1, blocking collectives, local(): packs = lax.all_gather(packed, 'col', axis=0)  6.02 us
    unnamed x16, local copies, waits for them, and re-layouts  5.37 us
    ppermute x1, waiting for transfers between devices, local(): recv_b = lax.ppermute(send_b, 'row', pairs_b)  3.7 us
    pallas_call x1, Pallas kernels, local(): pl.pallas_call(functools.partial(mid_kernel, (band_cols, cols_count, stri...  2.65 us
    ppermute x1, starting transfers between devices, local(): recv_b = lax.ppermute(send_b, 'row', pairs_b)  2.01 us
    ppermute x1, starting transfers between devices, local(): recv_a = lax.ppermute(send_a, 'row', pairs_a)  1.3 us
  transfers between devices with their start and end apart: 2, of which 2 were waited for; matrix products, arithmetic and copies ran while one was open for 0% of the time, Pallas kernels for 0%

profile of v1, /device:TPU:25, one launch (start us, length us, event | category | flops | bytes accessed | tf_op | source)
XLA Modules:
  0.0 39.0 jit_solution(2494587877365539410)
XLA Ops:
  0.6 0.0 copy-start
  0.6 0.9 %copy-done = f32[4,64,128]{2,1,0:T(8,128)S(1)} copy-done((f32[4,64,128]{2,1,0:T(8,128)S(1)}, f32[4,64,128]{2,1,0:T(8,128)}, u32[]{:S(2)}) %copy-start) | copy-done | bytes 131096
  1.5 0.0 copy-start.1
  1.5 0.8 %copy-done.1 = f32[2,64,128]{2,1,0:T(8,128)S(1)} copy-done((f32[2,64,128]{2,1,0:T(8,128)S(1)}, f32[2,64,128]{2,1,0:T(8,128)}, u32[]{:S(2)}) %copy-start.1) | copy-done | bytes 65560
  2.4 0.0 copy-start.2
  2.4 0.8 %copy-done.2 = f32[64,128]{1,0:T(8,128)S(1)} copy-done((f32[64,128]{1,0:T(8,128)S(1)}, f32[64,128]{1,0:T(8,128)}, u32[]{:S(2)}) %copy-start.2) | copy-done | bytes 32792
  3.1 0.0 copy-start.3
  3.1 0.8 %copy-done.3 = s32[64,128]{1,0:T(8,128)S(1)} copy-done((s32[64,128]{1,0:T(8,128)S(1)}, s32[64,128]{1,0:T(8,128)}, u32[]{:S(2)}) %copy-start.3) | copy-done | bytes 32792
  3.9 0.0 copy-start.4
  3.9 0.8 %copy-done.4 = s32[64,128]{1,0:T(8,128)S(1)} copy-done((s32[64,128]{1,0:T(8,128)S(1)}, s32[64,128]{1,0:T(8,128)}, u32[]{:S(2)}) %copy-start.4) | copy-done | bytes 32792
  4.7 0.0 copy-start.6
  4.7 0.7 %copy-done.6 = f32[4,128]{1,0:T(4,128)S(1)} copy-done((f32[4,128]{1,0:T(4,128)S(1)}, f32[4,128]{1,0:T(4,128)}, u32[]{:S(2)}) %copy-start.6) | copy-done | bytes 2072
  5.3 0.2 shard_map.118
  5.5 6.0 %all-gather = f32[320,128]{1,0:T(8,128)S(1)} all-gather(f32[80,128]{1,0:T(8,128)S(1)} %shard_map.118), channel_id=2, replica_groups=mesh['row'=8,'col'=4] {'col'}, dimensions={0}, use_global_device_ids=true | all-gather | bytes 204800 | tf_op jit(solution)/shard_map/all_gather | solution.py:507
  11.6 2.6 %shard_map.119 = (f32[6,64,128]{2,1,0:T(8,128)S(1)}, f32[64,128]{1,0:T(8,128)S(1)}, s32[64,128]{1,0:T(8,128)S(1)}, f32[15,8,128]{2,1,0:T(8,128)S(1)}, f32[15,8,128]{2,1,0:T(8,128)S(1)}, /*index=5*/f32[32,128]{1,0:T(8,128)S(1)}) custom-call(f32[64,128]{1,0:T(8,128)S(1)} %copy-done.2, f32[2,64,128]{2,1,0:T(8,128)S(1)} %copy-done.1, f32[4,64,128]{2,1,0:T(8,128)S(1)} %copy-done, ...), custom_call_target="tpu_custom_call" | custom-call | tf_op jit(solution)/shard_map/pallas_call | solution.py:516
  14.2 1.3 %collective-permute-start = (f32[15,8,128]{2,1,0:T(8,128)S(1)}, f32[15,8,128]{2,1,0:T(8,128)S(1)}, u32[]{:S(2)}, u32[]{:S(2)}) collective-permute-start(f32[15,8,128]{2,1,0:T(8,128)S(1)} %get-tuple-element.22), channel_id=1, source_target_pairs={{0,4},{4,0},{8,12},{12,8},{16,20},{20,16},{24,28},{28,24},{1,5},{5... | collective-permute-start | bytes 184328 | tf_op jit(solution)/shard_map/ppermute | solution.py:527
  15.5 2.0 %collective-permute-start.1 = (f32[15,8,128]{2,1,0:T(8,128)S(1)}, f32[15,8,128]{2,1,0:T(8,128)S(1)}, u32[]{:S(2)}, u32[]{:S(2)}) collective-permute-start(f32[15,8,128]{2,1,0:T(8,128)S(1)} %get-tuple-element.23), channel_id=1, source_target_pairs={{4,8},{8,4},{12,16},{16,12},{20,24},{24,20},{5,9},{9,5},{13,17},{1... | collective-permute-start | bytes 184328 | tf_op jit(solution)/shard_map/ppermute | solution.py:528
  17.5 0.1 collective-permute-done.recv_a
  17.7 3.7 %collective-permute-done.1.recv_b = f32[15,8,128]{2,1,0:T(8,128)S(1)} collective-permute-done((f32[15,8,128]{2,1,0:T(8,128)S(1)}, f32[15,8,128]{2,1,0:T(8,128)S(1)}, u32[]{:S(2)}, u32[]{:S(2)}) %collective-permute-start.1) | collective-permute-done | bytes 61472 | tf_op jit(solution)/shard_map/ppermute | solution.py:528
  21.4 0.7 %copy-done.7 = f32[3,4]{1,0:T(4,128)S(1)} copy-done((f32[3,4]{1,0:T(4,128)S(1)}, f32[3,4]{1,0:T(4,128)}, u32[]{:S(2)}) %copy-start.7) | copy-done | bytes 72
  22.0 9.2 %shard_map.120 = (f32[64,128]{1,0:T(8,128)}, f32[2,64,128]{2,1,0:T(8,128)}, f32[4,64,128]{2,1,0:T(8,128)}, f32[64,128]{1,0:T(8,128)S(1)}) custom-call(f32[64,128]{1,0:T(8,128)S(1)} %copy-done.2, f32[2,64,128]{2,1,0:T(8,128)S(1)} %copy-done.1, f32[4,64,128]{2,1,0:T(8,128)S(1)} %copy-done, s32[64,128]{1,0:T(8,128)S(1)} %copy-done.3, ...), custom_call_target="tpu_custom_call" | custom-call | tf_op jit(solution)/shard_map/pallas_call | solution.py:533
  31.2 7.0 %all-gather.1 = f32[256,128]{1,0:T(8,128)S(1)} all-gather(f32[64,128]{1,0:T(8,128)S(1)} %get-tuple-element.27), channel_id=3, replica_groups=mesh['row'=8,'col'=4] {'col'}, dimensions={0}, use_global_device_ids=true | all-gather | bytes 163840 | tf_op jit(solution)/shard_map/all_gather | solution.py:547
  38.2 0.0 copy-done.5
  38.2 0.8 %shard_map.121 = (f32[4,128]{1,0:T(4,128)}, f32[4,4,128]{2,1,0:T(4,128)}, f32[64,128]{1,0:T(8,128)}) custom-call(f32[4,64,128]{2,1,0:T(8,128)S(1)} %bitcast.3, f32[32,128]{1,0:T(8,128)S(1)} %get-tuple-element.28.bed, s32[64,128]{1,0:T(8,128)S(1)} %copy-done.5), custom_call_target="tpu_custom_call" | custom-call | tf_op jit(solution)/shard_map/pallas_call | solution.py:562
  (2 shorter events, 0.0 us)
Async XLA Ops:
  0.6 0.9 %copy-start = (f32[4,64,128]{2,1,0:T(8,128)S(1)}, f32[4,64,128]{2,1,0:T(8,128)}, u32[]{:S(2)}) copy-start(f32[4,64,128]{2,1,0:T(8,128)} %mud.5) | copy-start | bytes 393220
  1.5 0.8 %copy-start.1 = (f32[2,64,128]{2,1,0:T(8,128)S(1)}, f32[2,64,128]{2,1,0:T(8,128)}, u32[]{:S(2)}) copy-start(f32[2,64,128]{2,1,0:T(8,128)} %flow.5) | copy-start | bytes 196612
  2.4 0.8 %copy-start.2 = (f32[64,128]{1,0:T(8,128)S(1)}, f32[64,128]{1,0:T(8,128)}, u32[]{:S(2)}) copy-start(f32[64,128]{1,0:T(8,128)} %depth.5) | copy-start | bytes 98308
  3.1 0.8 %copy-start.3 = (s32[64,128]{1,0:T(8,128)S(1)}, s32[64,128]{1,0:T(8,128)}, u32[]{:S(2)}) copy-start(s32[64,128]{1,0:T(8,128)} %wet.5) | copy-start | bytes 98308
  3.9 0.8 %copy-start.4 = (s32[64,128]{1,0:T(8,128)S(1)}, s32[64,128]{1,0:T(8,128)}, u32[]{:S(2)}) copy-start(s32[64,128]{1,0:T(8,128)} %cells.5) | copy-start | bytes 98308
  4.7 0.7 %copy-start.6 = (f32[4,128]{1,0:T(4,128)S(1)}, f32[4,128]{1,0:T(4,128)}, u32[]{:S(2)}) copy-start(f32[4,128]{1,0:T(4,128)} %strip.1) | copy-start | bytes 6148
  14.2 3.5 %collective-permute-start = (f32[15,8,128]{2,1,0:T(8,128)S(1)}, f32[15,8,128]{2,1,0:T(8,128)S(1)}, u32[]{:S(2)}, u32[]{:S(2)}) collective-permute-start(f32[15,8,128]{2,1,0:T(8,128)S(1)} %get-tuple-element.22), channel_id=1, source_target_pairs={{0,4},{4,0},{8,12},{12,8},{16,20},{20,16},{24,28},{28,24},{1,5},{5... | collective-permute-start | bytes 184328 | tf_op jit(solution)/shard_map/ppermute | solution.py:527
  15.5 5.9 %collective-permute-start.1 = (f32[15,8,128]{2,1,0:T(8,128)S(1)}, f32[15,8,128]{2,1,0:T(8,128)S(1)}, u32[]{:S(2)}, u32[]{:S(2)}) collective-permute-start(f32[15,8,128]{2,1,0:T(8,128)S(1)} %get-tuple-element.23), channel_id=1, source_target_pairs={{4,8},{8,4},{12,16},{16,12},{20,24},{24,20},{5,9},{9,5},{13,17},{1... | collective-permute-start | bytes 184328 | tf_op jit(solution)/shard_map/ppermute | solution.py:528
  21.4 0.7 %copy-start.7 = (f32[3,4]{1,0:T(4,128)S(1)}, f32[3,4]{1,0:T(4,128)}, u32[]{:S(2)}) copy-start(f32[3,4]{1,0:T(4,128)} %params.1) | copy-start | bytes 148
  31.2 7.0 %copy-start.5 = (s32[64,128]{1,0:T(8,128)S(1)}, s32[64,128]{1,0:T(8,128)}, u32[]{:S(2)}) copy-start(s32[64,128]{1,0:T(8,128)} %cells.5) | copy-start | bytes 98308

commit v2 on v1

v2 whole, which is shorter than its diff:
```python
import functools

import jax
import jax.numpy as jnp
from jax import lax
from jax.experimental import pallas as pl
from jax.experimental.pallas import tpu as pltpu
from jax.sharding import PartitionSpec as P

SUBSTEPS = 4
LANES = 128
SUB = 8
UNROLL = 2
AHEAD = 1
TOP = SUB
RIM = 2 * SUBSTEPS

gravity = 1.0
time_step = 0.2
depth_floor = 1.25
drag_coeff = 0.02
settle_base = 0.05
critical_base = 0.05
erode_base = 0.002
exner_factor = 400.0


def vmem():
    return pl.BlockSpec(memory_space=pltpu.VMEM)


def smem():
    return pl.BlockSpec(memory_space=pltpu.SMEM)


def lane_ids(shape):
    return lax.broadcasted_iota(jnp.int32, shape, len(shape) - 1)


def params_of(limit=16 << 20):
    return pltpu.CompilerParams(vmem_limit_bytes=limit)


def pick(table, index):
    return jnp.take_along_axis(table, index, axis=1, mode="promise_in_bounds")


def hbm():
    return pl.BlockSpec(memory_space=pltpu.HBM)


def turn(x, shift):
    shift = shift % LANES
    return pltpu.roll(x, shift, 1) if shift else x


def folded_rows(rows):
    return -(-rows // SUB // (LANES // (2 * RIM)))


def pack_kernel(depth, flow, mud, wet, cells, strip, params, planes, coeffs, out, wet_ref, cell_ref, strip_ref, param_ref, sems):
    rows = depth.shape[0]
    fractions = mud.shape[0]
    moves = [
        (depth, planes.at[0]), (flow, planes.at[pl.ds(1, 2)]), (mud, planes.at[pl.ds(3, fractions)]), (wet, wet_ref),
        (cells, cell_ref), (strip, strip_ref), (params, param_ref),
    ]
    copies = [pltpu.make_async_copy(src, dst, sems.at[k]) for k, (src, dst) in enumerate(moves)]
    for copy in copies:
        copy.start()
    for copy in copies:
        copy.wait()
    count = 5 + fractions
    lane = lane_ids((SUB, LANES))
    group = lane // RIM
    pairs = LANES // (2 * RIM)
    spare = [[None] * folded_rows(rows) for _ in range(pairs, count)]
    for block in range(rows // SUB):
        at = pl.ds(block * SUB, SUB)
        planes[count - 2, at, :] = wet_ref[at, :].astype(jnp.float32)
        planes[count - 1, at, :] = cell_ref[at, :].astype(jnp.float32)
        packed = None
        for p in range(count):
            x = planes[p, at, :]
            slot = p if p < pairs else block % pairs
            low, high = turn(x, 2 * RIM * slot), turn(x, 2 * RIM * slot + 2 * RIM)
            old = packed if p < pairs else spare[p - pairs][block // pairs]
            both = jnp.where(group == 2 * slot, low, high)
            new = both if old is None else jnp.where(group // 2 == slot, both, old)
            if p < pairs:
                packed = new
            else:
                spare[p - pairs][block // pairs] = new
        out[at, :] = packed
    start = rows
    for x in [x for p in spare for x in p]:
        out[pl.ds(start, SUB), :] = x
        start += SUB
    strip_rows = strip.shape[0]
    for chunk in range(strip.shape[1] // LANES):
        out[pl.ds(start + chunk * strip_rows, strip_rows), :] = strip_ref[:, chunk * LANES : (chunk + 1) * LANES]
    for c in range(3):
        each = []
        for k in range(fractions):
            value = jnp.full((SUB, LANES), param_ref[c, k], jnp.float32)
            value = (settle_base * value, 1.0 / (critical_base * value), erode_base * value)[c]
            coeffs[c, k, :, :] = value
            each.append(value)
        mixed = each[0]
        for k in range(1, fractions):
            mixed = jnp.where(lane // (4 * RIM) == k, each[k], mixed)
        coeffs[c, fractions, :, :] = mixed


def spread_rows(frame_ref, block, shift):
    first = SUB + block * (SUB // 4) + shift
    low = jnp.broadcast_to(frame_ref[pl.ds(first, 1), :], (SUB, LANES))
    high = jnp.broadcast_to(frame_ref[pl.ds(first + 1, 1), :], (SUB, LANES))
    sub = lax.broadcasted_iota(jnp.int32, (SUB, LANES), 0)
    return jnp.where(sub < 4, low, high)


def split_cells(cells, band_cols):
    row = jnp.floor((cells + 0.5) * (1.0 / band_cols))
    return row.astype(jnp.int32), (cells - row * band_cols).astype(jnp.int32)


def row_shift_of(cell_row, block):
    sub = lax.broadcasted_iota(jnp.int32, (SUB, LANES), 0)
    return cell_row - (block * (SUB // 4) + sub // 4)


def lookup(frame_ref, block, shift, column):
    found = pick(spread_rows(frame_ref, block, 0), column)
    below = pick(spread_rows(frame_ref, block, -1), column)
    above = pick(spread_rows(frame_ref, block, 1), column)
    return jnp.where(shift == 0, found, jnp.where(shift < 0, below, above))


def starts_of(col_at, band_cols):
    coarse_start = col_at * (LANES // 4)
    return coarse_start, 0 if band_cols == LANES else coarse_start - (LANES - LANES // 4) // 2


def fill_frame(frame_ref, rows_of):
    frame_ref[...] = jnp.zeros_like(frame_ref)
    for r0, value in rows_of:
        frame_ref[pl.ds(SUB + r0, value.shape[0]), :] = value


def side_maker(geometry, planes, packs, frame_ref):
    band_cols, cols_count = geometry[:2]
    count, rows = planes.shape[:2]
    fractions = count - 5
    col_at = lax.axis_index("col")
    coarse_start, frame_start = starts_of(col_at, band_cols)
    wet_at, cell_at = count - 2, count - 1
    pairs = LANES // (2 * RIM)
    lane = lane_ids((SUB, LANES))
    width = 4 * RIM
    inside = lane % width
    group = lane // width
    is_low = inside < RIM
    is_high = inside >= 3 * RIM
    is_first = inside < 2 * RIM
    has_low = jnp.where(col_at > 0, 1.0, 0.0)
    has_high = jnp.where(col_at < cols_count - 1, 1.0, 0.0)
    scale = jnp.where(is_low, has_low, jnp.where(is_high, has_high, 1.0))
    left = jnp.maximum(col_at - 1, 0)
    right = jnp.minimum(col_at + 1, cols_count - 1)

    def make(block):
        at = pl.ds(block * SUB, SUB)

        def gather_to(p, base):
            if p < pairs:
                source, slot = at, p
            else:
                source = pl.ds(rows + ((p - pairs) * folded_rows(rows) + block // pairs) * SUB, SUB)
                slot = block % pairs
            x = planes[p, at, :]
            low = turn(packs[left, source, :], base - 2 * RIM * slot - RIM)
            high = turn(packs[right, source, :], base + 3 * RIM - 2 * RIM * slot)
            own = jnp.where(is_first, turn(x, base + RIM), turn(x, base + 3 * RIM))
            return jnp.where(is_low, low, jnp.where(is_high, high, own))

        def for_all(p):
            x = gather_to(p, 0)
            x = jnp.where(lane < width, x, pltpu.roll(x, width, 1))
            return jnp.where(lane < 2 * width, x, pltpu.roll(x, 2 * width, 1)) * scale

        sides = [for_all(p) for p in range(3)]
        each = gather_to(3, 0)
        for k in range(1, fractions):
            each = jnp.where(group == k, gather_to(3 + k, k * width), each)
        sides.append(each * scale)
        sides.append(for_all(wet_at))
        side_row, side_col = split_cells(for_all(cell_at), band_cols)
        side_at = jnp.where(scale > 0.0, side_col - frame_start, 0)
        sides.append(lookup(frame_ref, block, row_shift_of(side_row, block), side_at) * scale)
        cell_row, cell_col = split_cells(planes[cell_at, at, :], band_cols)
        shift = row_shift_of(cell_row, block)
        bed = lookup(frame_ref, block, shift, cell_col - frame_start)
        return sides, bed, (shift + 1) * 7 + (cell_col - coarse_start - lane // 4 + 3)

    return make


def edge_kernel(geometry, planes, packs, *refs):
    _, cols_count, strip_rows, from_packs = geometry
    frame = None if from_packs else refs[0]
    send_a, send_b, code, frame_ref = refs[0 if from_packs else 1 :]
    count, rows = planes.shape[:2]
    pairs = LANES // (2 * RIM)
    strip_at = rows + (count - pairs) * folded_rows(rows) * SUB
    if from_packs:
        fill_frame(
            frame_ref, [(d * strip_rows, packs[d, pl.ds(strip_at, strip_rows), :]) for d in range(cols_count)]
        )
    else:
        fill_frame(frame_ref, [(0, frame[...])])
    make = side_maker(geometry, planes, packs, frame_ref)
    parity = lax.axis_index("row") % 2
    last = rows // SUB - 1
    done = [make(0), make(last)]
    for out, turned in ((send_a, parity == 1), (send_b, parity == 0)):
        for p in range(count + 6):
            first, final = [
                planes[p, pl.ds(b * SUB, SUB), :] if p < count - 1 else bed if p == count - 1 else sides[p - count]
                for b, (sides, bed, _) in zip((0, last), done)
            ]
            out[p, :, :] = jnp.where(turned, first, final)
    code[0, :, :] = done[0][2]
    code[1, :, :] = done[1][2]


def half_minmod(before, here, after):
    low = 0.5 * (here - before)
    high = 0.5 * (after - here)
    return jnp.maximum(jnp.minimum(low, high), jnp.minimum(jnp.maximum(low, high), 0.0))


def face_fluxes(lefts, rights, normal, half_open):
    speed_l = lefts[normal] * pl.reciprocal(jnp.maximum(lefts[0], depth_floor))
    speed_r = rights[normal] * pl.reciprocal(jnp.maximum(rights[0], depth_floor))
    wave = jnp.maximum(
        jnp.abs(speed_l) + jnp.sqrt(gravity * lefts[0]), jnp.abs(speed_r) + jnp.sqrt(gravity * rights[0])
    )
    to_l = half_open * (speed_l + wave)
    to_r = half_open * (speed_r - wave)
    out = [l * to_l + r * to_r for l, r in zip(lefts, rights)]
    out[normal] = out[normal] + (0.5 * gravity) * half_open * (lefts[0] * lefts[0] + rights[0] * rights[0])
    return out


def stepper(coeffs, q_main, q_side, static_main, static_side, slope_main, slope_side, flux_main, flux_side, exchanged):
    channels = q_main.shape[1]
    fractions = channels - 3
    lane = lane_ids((SUB, LANES))
    width = 4 * RIM
    first_lane = lane == 0
    last_lane = lane == LANES - 1
    wet_at, bed_at = 0, 1

    def coeffs_of(k):
        return [coeffs[c, k, :, :] for c in range(3)]

    def start_of(k):
        return max(k - 3, 0) * width

    def low_edge(x, k):
        return turn(x, 1 - RIM - start_of(k))

    def high_edge(x, k):
        return turn(x, LANES - 1 - 3 * RIM - start_of(k))

    def rows_at(ref, p, row):
        return ref[p, pl.ds(row, SUB), :]

    def statics(block):
        r0 = TOP + block * SUB
        for ref, is_main in ((static_side, False), (static_main, True)):
            w = rows_at(ref, wet_at, r0)
            b_plus = rows_at(ref, bed_at, r0 + 1)
            b_minus = rows_at(ref, bed_at, r0 - 1)
            b = rows_at(ref, bed_at, r0)
            w_right, b_right = pltpu.roll(w, LANES - 1, 1), pltpu.roll(b, LANES - 1, 1)
            b_left = pltpu.roll(b, 1, 1)
            if is_main:
                w_edge, b_edge = rows_at(static_side, wet_at, r0), rows_at(static_side, bed_at, r0)
                w_right = jnp.where(last_lane, high_edge(w_edge, 0), w_right)
                b_right = jnp.where(last_lane, high_edge(b_edge, 0), b_right)
                b_left = jnp.where(first_lane, low_edge(b_edge, 0), b_left)
            at = pl.ds(r0, SUB)
            ref[2, at, :] = 0.5 * (w * rows_at(ref, wet_at, r0 + 1))
            ref[3, at, :] = 0.5 * (w * w_right)
            ref[4, at, :] = (0.5 * gravity) * (b_plus - b_minus)
            ref[5, at, :] = (0.5 * gravity) * (b_right - b_left)
            ref[6, at, :] = time_step * w

    def slopes(block, level):
        r0 = pl.multiple_of(TOP + block * SUB, SUB)
        at = pl.ds(r0, SUB)
        for q, s, n in ((q_side, slope_side, 4), (q_main, slope_main, channels)):
            if n == 4 and level == SUBSTEPS - 1:
                continue
            q = q.at[level % 2]
            for k in range(n):
                s[k, at, :] = half_minmod(rows_at(q, k, r0 - 1), rows_at(q, k, r0), rows_at(q, k, r0 + 1))

    def row_fluxes(q, s, f, static, n, r0):
        lefts = [rows_at(q, k, r0) + rows_at(s, k, r0) for k in range(n)]
        rights = [rows_at(q, k, r0 + 1) - rows_at(s, k, r0 + 1) for k in range(n)]
        out = face_fluxes(lefts, rights, 1, rows_at(static, 2, r0))
        for k in range(n):
            f[k, pl.ds(r0, SUB), :] = out[k]
        return [rows_at(f, k, r0 - 1) - out[k] for k in range(n)]

    def col_fluxes(here, static, n, r0, edges):
        lefts, rights = [], []
        for k in range(n):
            before, after = pltpu.roll(here[k], 1, 1), pltpu.roll(here[k], LANES - 1, 1)
            if edges is not None:
                before = jnp.where(first_lane, low_edge(edges[min(k, 3)], k), before)
                after = jnp.where(last_lane, high_edge(edges[min(k, 3)], k), after)
            s = half_minmod(before, here[k], after)
            lefts.append(here[k] + s)
            rights.append(pltpu.roll(here[k] - s, LANES - 1, 1))
        return face_fluxes(lefts, rights, 2, rows_at(static, 3, r0))

    def update(here, net, static, coeffs, r0):
        step = rows_at(static, 6, r0)
        inv = pl.reciprocal(jnp.maximum(here[0], depth_floor))
        u, v = here[1] * inv, here[2] * inv
        squared = u * u + v * v + 1e-06
        drag = drag_coeff * jnp.sqrt(squared)
        new = [
            here[0] + step * net[0],
            here[1] + step * (net[1] - here[0] * rows_at(static, 4, r0) - drag * u),
            here[2] + step * (net[2] - here[0] * rows_at(static, 5, r0) - drag * v),
        ]
        changes = []
        for k in range(len(here) - 3):
            m = here[3 + k]
            settle, inv_critical, erode = coeffs[k]
            change = step * (settle * m * inv - erode * jnp.maximum(squared * inv_critical - 1.0, 0.0))
            changes.append(change)
            new.append(m + step * net[3 + k] - change)
        return new, changes

    def advance(block, level, rows_only=False):
        r0 = pl.multiple_of(TOP + block * SUB, SUB)
        at = pl.ds(r0, SUB)
        last = level == SUBSTEPS - 1
        qs, qm = q_side.at[level % 2], q_main.at[level % 2]
        slopes(block + 1, level)
        if rows_only:
            row_fluxes(qm, slope_main, flux_main, static_main, channels, r0)
            if not last:
                row_fluxes(qs, slope_side, flux_side, static_side, 4, r0)
            return
        edges = [rows_at(qs, k, r0) for k in range(4)]
        side_flux = col_fluxes(edges, static_side, 4, r0, None)
        if not last:
            net = row_fluxes(qs, slope_side, flux_side, static_side, 4, r0)
            net = [x + (pltpu.roll(f, 1, 1) - f) for x, f in zip(net, side_flux)]
            new, _ = update(edges, net, static_side, [coeffs_of(fractions)], r0)
            for k in range(4):
                q_side[(level + 1) % 2, k, at, :] = new[k]
        net = row_fluxes(qm, slope_main, flux_main, static_main, channels, r0)
        here = [rows_at(qm, k, r0) for k in range(channels)]
        fluxes = col_fluxes(here, static_main, channels, r0, edges)
        for k in range(channels):
            edge = side_flux[min(k, 3)]
            f = jnp.where(last_lane, turn(edge, LANES - 3 * RIM - start_of(k)), fluxes[k])
            net[k] = net[k] + (jnp.where(first_lane, low_edge(edge, k), pltpu.roll(fluxes[k], 1, 1)) - f)
        new, changes = update(here, net, static_main, [coeffs_of(k) for k in range(fractions)], r0)
        for k in range(channels):
            q_main[(level + 1) % 2, k, at, :] = new[k]
        for k in range(fractions):
            if level == 0:
                exchanged[k, at, :] = changes[k]
            else:
                exchanged[k, at, :] = exchanged[k, at, :] + changes[k]

    def sweep(first, end, level, unroll=None):
        def one(block, carry):
            advance(block, level)
            return carry

        if unroll is None:
            for block in range(first, end):
                advance(block, level)
        else:
            lax.fori_loop(first, end, one, 0, unroll=unroll)

    return statics, slopes, advance, sweep


def early_kernel(
    geometry, planes, packs, frame_ref, send_a, send_b, ends, coeffs,
    q_main, q_side, static_main, static_side, flux_main, flux_side, exchanged, code, slope_main, slope_side,
):
    count, rows = planes.shape[:2]
    channels = count - 2
    body = TOP + RIM
    parity = lax.axis_index("row") % 2
    blocks = rows // SUB
    for k in range(channels):
        q_main[0, k, pl.ds(body, rows), :] = planes[k]
    static_main[0, pl.ds(body, rows), :] = planes[channels]
    for block, is_first in ((0, True), (blocks - 1, False)):
        at = pl.ds(body + block * SUB, SUB)
        mine = [
            jnp.where((parity == 1) == is_first, send_a[p], send_b[p]) for p in range(channels + 1, channels + 8)
        ]
        static_main[1, at, :] = mine[0]
        for k in range(4):
            q_side[0, k, at, :] = mine[1 + k]
        static_side[0, at, :] = mine[5]
        static_side[1, at, :] = mine[6]
        code[pl.ds(block * SUB, SUB), :] = ends[0 if is_first else 1]
    make = side_maker(geometry, planes, packs, frame_ref)
    for block in range(1, blocks - 1):
        at = pl.ds(body + block * SUB, SUB)
        sides, bed, coded = make(block)
        static_main[1, at, :] = bed
        for k in range(4):
            q_side[0, k, at, :] = sides[k]
        static_side[0, at, :] = sides[4]
        static_side[1, at, :] = sides[5]
        code[pl.ds(block * SUB, SUB), :] = coded
    statics, slopes, advance, sweep = stepper(
        coeffs, q_main, q_side, static_main, static_side, slope_main, slope_side, flux_main, flux_side, exchanged
    )
    total = blocks + 2
    for block in range(1, total - 2):
        statics(block)
    for level in range(AHEAD):
        slopes(1 + level, level)
        advance(1 + level, level, rows_only=True)
        sweep(2 + level, total - 2 - level, level, UNROLL)


def late_kernel(
    band_cols, recv_a, recv_b, coeffs, code,
    q_main_in, q_side_in, static_main_in, static_side_in, flux_main_in, flux_side_in, exchanged_in,
    depth_out, flow_out, mud_out, partial,
    q_main, q_side, static_main, static_side, flux_main, flux_side, exchanged,
    slope_main, slope_side, sems,
):
    del q_main_in, q_side_in, static_main_in, static_side_in, flux_main_in, flux_side_in, exchanged_in
    rows = code.shape[0]
    channels = q_main.shape[1]
    fractions = channels - 3
    body = TOP + RIM
    parity = lax.axis_index("row") % 2
    total = rows // SUB + 2

    def fill(put, p):
        a, b = recv_a[p], recv_b[p]
        put(pl.ds(TOP, RIM), jnp.where(parity == 1, a, b))
        put(pl.ds(body + rows, RIM), jnp.where(parity == 1, b, a))

    for k in range(channels + 8):
        def put(at, x, k=k):
            if k < channels:
                q_main[0, k, at, :] = x
            elif k < channels + 2:
                static_main[k - channels, at, :] = x
            elif k < channels + 6:
                q_side[0, k - channels - 2, at, :] = x
            else:
                static_side[k - channels - 6, at, :] = x

        fill(put, k)
    statics, slopes, advance, sweep = stepper(
        coeffs, q_main, q_side, static_main, static_side, slope_main, slope_side, flux_main, flux_side, exchanged
    )
    for block in (0, total - 2, total - 1):
        statics(block)
    if total > 3:
        statics(1)
    for level in range(SUBSTEPS):
        slopes(0, level)
        if level < AHEAD:
            sweep(0, 2 + level, level)
            slopes(total - 2 - level, level)
            sweep(total - 2 - level, total, level)
        elif level < SUBSTEPS - 1:
            sweep(0, total, level, UNROLL)
        else:
            advance(0, level, rows_only=True)
            sweep(1, total - 1, level, UNROLL)
    final = q_main.at[SUBSTEPS % 2]
    here = pl.ds(body, rows)
    copies = [pltpu.make_async_copy(final.at[0, here], depth_out, sems.at[0])]
    copies.append(pltpu.make_async_copy(final.at[pl.ds(1, 2), here], flow_out, sems.at[1]))
    copies.append(pltpu.make_async_copy(final.at[pl.ds(3, fractions), here], mud_out, sems.at[2]))
    for copy in copies:
        copy.start()

    coarse_rows = rows // 4
    parts = [[exchanged[f, pl.ds(body + k, coarse_rows, stride=4), :] for k in range(4)] for f in range(fractions)]
    codes = [code[pl.ds(k, coarse_rows, stride=4), :] for k in range(4)]
    to_coarse = (
        lax.broadcasted_iota(jnp.int32, (LANES, LANES), 0) // 4 == lax.broadcasted_iota(jnp.int32, (LANES, LANES), 1)
    ).astype(jnp.bfloat16)
    coarse_start, frame_start = starts_of(lax.axis_index("col"), band_cols)
    moved_total = None
    for col_shift in range(7):
        sums = [None] * fractions
        for row_shift in range(3):
            hits = [c == row_shift * 7 + col_shift for c in codes]
            for f in range(fractions):
                part = None
                for k in range(4):
                    x = jnp.where(hits[k], parts[f][k], 0.0)
                    part = x if part is None else part + x
                if row_shift != 1:
                    part = pltpu.roll(part, 1 if row_shift == 2 else coarse_rows - 1, 0)
                sums[f] = part if sums[f] is None else sums[f] + part
        rest = jnp.concatenate(sums, axis=0)
        z = None
        for _ in range(3):
            term = rest.astype(jnp.bfloat16)
            rest = rest - term.astype(jnp.float32)
            moved = jnp.dot(term, to_coarse, preferred_element_type=jnp.float32)
            z = moved if z is None else z + moved
        z = pltpu.roll(z, (coarse_start - frame_start + col_shift - 3 + LANES) % LANES, 1)
        moved_total = z if moved_total is None else moved_total + z
    partial[...] = moved_total
    for copy in copies:
        copy.wait()


def bed_kernel(geometry, sums, bed, planes, bed_out, deposit_out, fine, frame_ref, total_ref):
    band_cols, cols_count, strip_rows = geometry
    cells = planes.at[planes.shape[0] - 1]
    rows = cells.shape[0]
    band_rows = rows // 4
    fractions = sums.shape[1] // band_rows
    total = sums[0]
    for d in range(1, cols_count):
        total = total + sums[d]
    total_ref[...] = (exner_factor / 16.0) * total
    at = lax.axis_index("col") * strip_rows
    frame_ref[...] = jnp.zeros_like(frame_ref)
    whole = None
    for f in range(fractions):
        part = total_ref[pl.ds(f * band_rows, band_rows), :]
        whole = part if whole is None else whole + part
        deposit_out[f, :, :] = total_ref[pl.ds(f * band_rows + at, strip_rows), :]
    frame_ref[pl.ds(SUB, band_rows), :] = bed[pl.ds(SUB, band_rows), :] + whole
    bed_out[...] = frame_ref[pl.ds(SUB + at, strip_rows), :]
    for block in range(rows // SUB):
        here = pl.ds(block * SUB, SUB)
        cell_row, cell_col = split_cells(cells[here, :], band_cols)
        fine[here, :] = lookup(frame_ref, block, row_shift_of(cell_row, block), cell_col)


def local(water_depth, discharge, sediment, bed_level, cell_map, wet_mask, sediment_params):
    tile_rows, tile_cols = water_depth.shape
    fractions = sediment.shape[0]
    strip_rows, band_cols = bed_level.shape
    cols_count = lax.axis_size("col")
    rows_count = lax.axis_size("row")
    band_rows = tile_rows // 4
    f32 = functools.partial(jax.ShapeDtypeStruct, dtype=jnp.float32)
    narrow = band_cols == LANES
    col_at = lax.axis_index("col")
    frame_start = starts_of(col_at, band_cols)[1]
    chunks = band_cols // LANES
    extra = (5 + fractions - LANES // (2 * RIM)) * folded_rows(tile_rows) * SUB
    pack_rows = tile_rows + extra + -(-chunks * strip_rows // SUB) * SUB

    channels = 3 + fractions
    count = channels + 2
    space = functools.partial(pltpu.VMEM, dtype=jnp.float32)
    arguments = (water_depth, discharge, sediment, wet_mask, cell_map, bed_level, sediment_params)
    planes, coeffs, packed = pl.pallas_call(
        pack_kernel,
        out_shape=(
            f32((count, tile_rows, LANES)), f32((3, fractions + 1, SUB, LANES)), f32((pack_rows, LANES)),
        ),
        in_specs=[hbm()] * 7, out_specs=(vmem(),) * 3, compiler_params=params_of(),
        scratch_shapes=[
            pltpu.VMEM((tile_rows, LANES), jnp.int32), pltpu.VMEM((tile_rows, LANES), jnp.int32),
            space(bed_level.shape), pltpu.SMEM(sediment_params.shape, jnp.float32), pltpu.SemaphoreType.DMA((7,)),
        ],
    )(*[pltpu.with_memory_space_constraint(x, pltpu.HBM) for x in arguments])
    packs = lax.all_gather(packed, "col", axis=0)

    frames = []
    if not narrow:
        strips = packs[:, tile_rows + extra : tile_rows + extra + chunks * strip_rows]
        band = strips.reshape(cols_count, chunks, strip_rows, LANES).transpose(0, 2, 1, 3).reshape(band_rows, band_cols)
        wide = jnp.pad(band, ((0, 0), (LANES, LANES)))
        frames = [lax.dynamic_slice(wide, (jnp.int32(0), frame_start + LANES), (band_rows, LANES))]
    geometry = (band_cols, cols_count, strip_rows, narrow)
    send_a, send_b, ends, framed = pl.pallas_call(
        functools.partial(edge_kernel, geometry),
        out_shape=(
            f32((count + 6, SUB, LANES)), f32((count + 6, SUB, LANES)),
            jax.ShapeDtypeStruct((2, SUB, LANES), jnp.int32), f32((band_rows + 2 * SUB, LANES)),
        ),
        in_specs=[vmem()] * (2 + len(frames)), out_specs=(vmem(),) * 4, compiler_params=params_of(),
    )(planes, packs, *frames)

    pairs_a = [p for i in range(0, rows_count - 1, 2) for p in ((i, i + 1), (i + 1, i))]
    pairs_b = [p for i in range(1, rows_count - 1, 2) for p in ((i, i + 1), (i + 1, i))]
    recv_a = lax.ppermute(send_a, "row", pairs_a)
    recv_b = lax.ppermute(send_b, "row", pairs_b)

    span = tile_rows + 2 * RIM + 3 * SUB
    state = (
        f32((2, channels, span, LANES)), f32((2, 4, span, LANES)), f32((7, span, LANES)), f32((7, span, LANES)),
        f32((channels, span, LANES)), f32((4, span, LANES)), f32((fractions, span, LANES)),
    )
    slope_space = [space((channels, span, LANES)), space((4, span, LANES))]
    *begun, code = pl.pallas_call(
        functools.partial(early_kernel, geometry),
        out_shape=(*state, jax.ShapeDtypeStruct((tile_rows, LANES), jnp.int32)),
        in_specs=[vmem()] * 7, out_specs=(vmem(),) * 8, compiler_params=params_of(), scratch_shapes=slope_space,
    )(planes, packs, framed, send_a, send_b, ends, coeffs)
    depth_out, discharge_out, sediment_out, partial = pl.pallas_call(
        functools.partial(late_kernel, band_cols),
        out_shape=(
            f32(water_depth.shape), f32(discharge.shape), f32(sediment.shape), f32((fractions * band_rows, LANES)),
            *state,
        ),
        in_specs=[vmem()] * 11, out_specs=(hbm(),) * 3 + (vmem(),) * 8, compiler_params=params_of(),
        input_output_aliases={4 + k: 4 + k for k in range(7)},
        scratch_shapes=[*slope_space, pltpu.SemaphoreType.DMA((3,))],
    )(recv_a, recv_b, coeffs, code, *begun)[:4]

    sums = lax.all_gather(partial, "col", axis=0)
    geometry = (band_cols if narrow else LANES, cols_count, strip_rows)
    if narrow:
        look_cells = planes
    else:
        wide = jnp.zeros((fractions, band_rows, band_cols + 2 * LANES), jnp.float32)
        for d in range(cols_count):
            start = LANES + d * (tile_cols // 4) - (LANES - tile_cols // 4) // 2
            wide = wide.at[:, :, start : start + LANES].add(sums[d].reshape(fractions, band_rows, LANES))
        share = lax.dynamic_slice_in_dim(wide, col_at * strip_rows, strip_rows, axis=1)[:, :, LANES:-LANES]
        deposit_wide = exner_factor / 16.0 * share
        bed_wide = bed_level + jnp.sum(deposit_wide, axis=0)
        sums = lax.dynamic_slice_in_dim(wide, frame_start + LANES, LANES, axis=2).reshape(1, -1, LANES)
        geometry = (LANES, 1, strip_rows)
        look_cells = (cell_map // band_cols * LANES + cell_map % band_cols - frame_start).astype(jnp.float32)[None]
    bed_new, deposit, fine_bed = pl.pallas_call(
        functools.partial(bed_kernel, geometry),
        out_shape=(f32((strip_rows, LANES)), f32((fractions, strip_rows, LANES)), f32((tile_rows, LANES))),
        in_specs=[vmem()] * 3, out_specs=(vmem(),) * 3, compiler_params=params_of(),
        scratch_shapes=[space((band_rows + 2 * SUB, LANES)), space((fractions * band_rows, LANES))],
    )(sums, framed, look_cells)
    if not narrow:
        bed_new, deposit = bed_wide, deposit_wide
    return (depth_out, discharge_out, sediment_out, fine_bed, bed_new, deposit)


def solution(mesh):
    placed = (
        P("row", "col"),
        P(None, "row", "col"),
        P(None, "row", "col"),
        P(("row", "col"), None),
        P("row", "col"),
        P("row", "col"),
        P(),
    )
    return jax.shard_map(
        local,
        mesh=mesh,
        in_specs=placed,
        out_specs=(
            P("row", "col"),
            P(None, "row", "col"),
            P(None, "row", "col"),
            P("row", "col"),
            P(("row", "col"), None),
            P(None, ("row", "col"), None),
        ),
        check_vma=False,
    )
```

time: 39.5 us -> 31.4 us (0.79); the launches traced: 39 us -> 31.3 us
  local copies, waits for them, and re-layouts: 5.37 us -> 0 us
  waiting for transfers between devices: 3.83 us -> 0.54 us
  Pallas kernels: 12.8 us -> 13.9 us
    unnamed x16 -> x0, local copies, waits for them, and re-layouts: 5.37 us -> none
    ppermute x1, waiting for transfers between devices: 3.7 us -> 0.53 us  [local(): recv_b = lax.ppermute(send_b, 'row', pairs_b)]
    pallas_call x3 -> x4, Pallas kernels: 12 us -> 13.1 us  [the longest x1 8.29 us: local(): pl.pallas_call(functools.partial(late_kernel, band_cols), out_shape=(f32(...]
  transfers between devices with their start and end apart: 2 -> 2, of which waited for: 2 -> 1; matrix products, arithmetic and copies ran while one was open for 0% -> 0% of each run, Pallas kernels for 0% -> 10%
where the time goes in v2:
time: 31.4 us; the launch traced here: 31.3 us
  Pallas kernels  13.9 us (44%)
  blocking collectives  12.9 us (41%)
  starting transfers between devices  3.31 us (11%)
  between operations  0.68 us (2%)
  waiting for transfers between devices  0.54 us (2%)
    pallas_call x1, Pallas kernels, local(): pl.pallas_call(functools.partial(late_kernel, band_cols), out_shape=(f32(...  8.29 us
    all_gather x1, blocking collectives, local(): sums = lax.all_gather(partial, 'col', axis=0)  6.85 us
    all_gather x1, blocking collectives, local(): packs = lax.all_gather(packed, 'col', axis=0)  6.02 us
    pallas_call x1, Pallas kernels, local(): pl.pallas_call(functools.partial(early_kernel, geometry), out_shape=(*sta...  3.29 us
    ppermute x1, starting transfers between devices, local(): recv_b = lax.ppermute(send_b, 'row', pairs_b)  2.01 us
    ppermute x1, starting transfers between devices, local(): recv_a = lax.ppermute(send_a, 'row', pairs_a)  1.3 us
    pallas_call x1, Pallas kernels, local(): pl.pallas_call(pack_kernel, out_shape=(f32((count, tile_rows, LANES)), f3...  1.24 us
    pallas_call x1, Pallas kernels, local(): pl.pallas_call(functools.partial(bed_kernel, geometry), out_shape=(f32((s...  0.75 us
  transfers between devices with their start and end apart: 2, of which 1 were waited for; matrix products, arithmetic and copies ran while one was open for 0% of the time, Pallas kernels for 10%

profile of v2, /device:TPU:25, one launch (start us, length us, event | category | flops | bytes accessed | tf_op | source)
XLA Modules:
  0.0 31.3 jit_solution(18280973248212367742)
XLA Ops:
  0.6 1.2 %shard_map.118 = (f32[9,64,128]{2,1,0:T(8,128)S(1)}, f32[3,5,8,128]{3,2,1,0:T(8,128)S(1)}, f32[80,128]{1,0:T(8,128)S(1)}) custom-call(f32[64,128]{1,0:T(8,128)} %depth.1, f32[2,64,128]{2,1,0:T(8,128)} %flow.1, f32[4,64,128]{2,1,0:T(8,128)} %mud.1, s32[64,128]{1,0:T(8,128)} %wet.1, s32[64,128]{1,0:T(8,128)} %cells.1, f32[4,128]{1,0:T(4,128)} %strip.1, ...), custom_call_target="tpu_custom_call" | custom-call | tf_op jit(solution)/shard_map/pallas_call | solution.py:581
  1.9 6.0 %all-gather = f32[320,128]{1,0:T(8,128)S(1)} all-gather(f32[80,128]{1,0:T(8,128)S(1)} %get-tuple-element.29), channel_id=2, replica_groups=mesh['row'=8,'col'=4] {'col'}, dimensions={0}, use_global_device_ids=true | all-gather | bytes 204800 | tf_op jit(solution)/shard_map/all_gather | solution.py:592
  7.9 0.3 %shard_map.119 = (f32[15,8,128]{2,1,0:T(8,128)S(1)}, f32[15,8,128]{2,1,0:T(8,128)S(1)}, s32[2,8,128]{2,1,0:T(8,128)S(1)}, f32[32,128]{1,0:T(8,128)S(1)}) custom-call(f32[9,64,128]{2,1,0:T(8,128)S(1)} %get-tuple-element.28.planes, f32[4,80,128]{2,1,0:T(8,128)S(1)} %bitcast.2), custom_call_target="tpu_custom_call" | custom-call | tf_op jit(solution)/shard_map/pallas_call | solution.py:601
  8.2 1.3 %collective-permute-start = (f32[15,8,128]{2,1,0:T(8,128)S(1)}, f32[15,8,128]{2,1,0:T(8,128)S(1)}, u32[]{:S(2)}, u32[]{:S(2)}) collective-permute-start(f32[15,8,128]{2,1,0:T(8,128)S(1)} %get-tuple-element.30.send_a), channel_id=1, source_target_pairs={{0,4},{4,0},{8,12},{12,8},{16,20},{20,16},{24,28},{28,24},{1,5},{5... | collective-permute-start | bytes 184328 | tf_op jit(solution)/shard_map/ppermute | solution.py:612
  9.5 2.0 %collective-permute-start.1 = (f32[15,8,128]{2,1,0:T(8,128)S(1)}, f32[15,8,128]{2,1,0:T(8,128)S(1)}, u32[]{:S(2)}, u32[]{:S(2)}) collective-permute-start(f32[15,8,128]{2,1,0:T(8,128)S(1)} %get-tuple-element.31.send_b), channel_id=1, source_target_pairs={{4,8},{8,4},{12,16},{16,12},{20,24},{24,20},{5,9},{9,5},{13,17},{1... | collective-permute-start | bytes 184328 | tf_op jit(solution)/shard_map/ppermute | solution.py:613
  11.5 3.3 %shard_map.120 = (f32[2,7,104,128]{3,2,1,0:T(8,128)S(1)}, f32[2,4,104,128]{3,2,1,0:T(8,128)S(1)}, f32[7,104,128]{2,1,0:T(8,128)S(1)}, f32[7,104,128]{2,1,0:T(8,1...) custom-call(f32[9,64,128]{2,1,0:T(8,128)S(1)} %get-tuple-element.28., ...), custom_call_target="tpu_custom_call" | custom-call | tf_op jit(solution)/shard_map/pallas_call | solution.py:621
  14.8 0.0 collective-permute-done.recv_a
  14.8 0.5 %collective-permute-done.1.recv_b = f32[15,8,128]{2,1,0:T(8,128)S(1)} collective-permute-done((f32[15,8,128]{2,1,0:T(8,128)S(1)}, f32[15,8,128]{2,1,0:T(8,128)S(1)}, u32[]{:S(2)}, u32[]{:S(2)}) %collective-permute-start.1) | collective-permute-done | bytes 61472 | tf_op jit(solution)/shard_map/ppermute | solution.py:613
  15.4 8.3 %shard_map.121 = (f32[64,128]{1,0:T(8,128)}, f32[2,64,128]{2,1,0:T(8,128)}, f32[4,64,128]{2,1,0:T(8,128)}, f32[64,128]{1,0:T(8,128)S(1)}, f32[2,7,104,128]{3,2,1...) custom-call(f32[15,8,128]{2,1,0:T(8,128)S(1)} %collective-permute-do, ...), custom_call_target="tpu_custom_call", output_to_operand_aliasing={{4}: (4, {}), {5}: (5, {}), {6}: (6, {}), {7}: (7, {}), {8}... | custom-call | tf_op jit(solution)/shard_map/pallas_call | solution.py:626
  23.7 6.8 %all-gather.1 = f32[256,128]{1,0:T(8,128)S(1)} all-gather(f32[64,128]{1,0:T(8,128)S(1)} %get-tuple-element.46), channel_id=3, replica_groups=mesh['row'=8,'col'=4] {'col'}, dimensions={0}, use_global_device_ids=true | all-gather | bytes 163840 | tf_op jit(solution)/shard_map/all_gather | solution.py:637
  30.5 0.8 %shard_map.122 = (f32[4,128]{1,0:T(4,128)}, f32[4,4,128]{2,1,0:T(4,128)}, f32[64,128]{1,0:T(8,128)}) custom-call(f32[4,64,128]{2,1,0:T(8,128)S(1)} %bitcast.4, f32[32,128]{1,0:T(8,128)S(1)} %get-tuple-element.33.frame_ref.bed, f32[9,64,128]{2,1,0:T(8,128)S(1)} %get-tuple-element.28.planes), custom_call_target="tpu_custom_call" | custom-call | tf_op jit(solution)/shard_map/pallas_call | solution.py:652
Async XLA Ops:
  8.2 6.6 %collective-permute-start = (f32[15,8,128]{2,1,0:T(8,128)S(1)}, f32[15,8,128]{2,1,0:T(8,128)S(1)}, u32[]{:S(2)}, u32[]{:S(2)}) collective-permute-start(f32[15,8,128]{2,1,0:T(8,128)S(1)} %get-tuple-element.30.send_a), channel_id=1, source_target_pairs={{0,4},{4,0},{8,12},{12,8},{16,20},{20,16},{24,28},{28,24},{1,5},{5... | collective-permute-start | bytes 184328 | tf_op jit(solution)/shard_map/ppermute | solution.py:612
  9.5 5.9 %collective-permute-start.1 = (f32[15,8,128]{2,1,0:T(8,128)S(1)}, f32[15,8,128]{2,1,0:T(8,128)S(1)}, u32[]{:S(2)}, u32[]{:S(2)}) collective-permute-start(f32[15,8,128]{2,1,0:T(8,128)S(1)} %get-tuple-element.31.send_b), channel_id=1, source_target_pairs={{4,8},{8,4},{12,16},{16,12},{20,24},{24,20},{5,9},{9,5},{13,17},{1... | collective-permute-start | bytes 184328 | tf_op jit(solution)/shard_map/ppermute | solution.py:613

commit v3 on v2

--- a/solution.py
+++ b/solution.py
@@ -10,9 +10,11 @@
 SUBSTEPS = 4
 LANES = 128
 SUB = 8
-UNROLL = 2
+GROUP = 1
+STRAIGHT = 12
 AHEAD = 1
 TOP = SUB
+SMALLEST = 1.1754944e-38
 RIM = 2 * SUBSTEPS
 
 gravity = 1.0
@@ -99,11 +101,15 @@
     strip_rows = strip.shape[0]
     for chunk in range(strip.shape[1] // LANES):
         out[pl.ds(start + chunk * strip_rows, strip_rows), :] = strip_ref[:, chunk * LANES : (chunk + 1) * LANES]
+    by_param = [
+        [jnp.full((SUB, LANES), param_ref[c, k], jnp.float32) for k in range(fractions)] for c in range(3)
+    ]
     for c in range(3):
         each = []
         for k in range(fractions):
-            value = jnp.full((SUB, LANES), param_ref[c, k], jnp.float32)
-            value = (settle_base * value, 1.0 / (critical_base * value), erode_base * value)[c]
+            settle, critical, erode = [by_param[n][k] for n in range(3)]
+            erode = erode_base * erode
+            value = (settle_base * settle, erode / (critical_base * critical), erode)[c]
             coeffs[c, k, :, :] = value
             each.append(value)
         mixed = each[0]
@@ -235,16 +241,20 @@
 
 
 def half_minmod(before, here, after):
-    low = 0.5 * (here - before)
-    high = 0.5 * (after - here)
-    return jnp.maximum(jnp.minimum(low, high), jnp.minimum(jnp.maximum(low, high), 0.0))
+    low = here - before
+    high = after - here
+    return 0.5 * jnp.maximum(jnp.minimum(low, high), jnp.minimum(jnp.maximum(low, high), 0.0))
+
+
+def root(x):
+    return x * lax.rsqrt(jnp.maximum(x, SMALLEST))
 
 
 def face_fluxes(lefts, rights, normal, half_open):
     speed_l = lefts[normal] * pl.reciprocal(jnp.maximum(lefts[0], depth_floor))
     speed_r = rights[normal] * pl.reciprocal(jnp.maximum(rights[0], depth_floor))
     wave = jnp.maximum(
-        jnp.abs(speed_l) + jnp.sqrt(gravity * lefts[0]), jnp.abs(speed_r) + jnp.sqrt(gravity * rights[0])
+        jnp.abs(speed_l) + root(gravity * lefts[0]), jnp.abs(speed_r) + root(gravity * rights[0])
     )
     to_l = half_open * (speed_l + wave)
     to_r = half_open * (speed_r - wave)
@@ -253,8 +263,11 @@
     return out
 
 
-def stepper(coeffs, q_main, q_side, static_main, static_side, slope_main, slope_side, flux_main, flux_side, exchanged):
-    channels = q_main.shape[1]
+def stepper(
+    coeffs, q_main, q_side, static_main, static_side, flux_main, flux_side, exchanged,
+    slope_main, slope_side, low_main, high_main, low_side, high_side, cross_main, cross_side,
+):
+    channels = q_main[0].shape[0]
     fractions = channels - 3
     lane = lane_ids((SUB, LANES))
     width = 4 * RIM
@@ -298,15 +311,13 @@
             ref[5, at, :] = (0.5 * gravity) * (b_right - b_left)
             ref[6, at, :] = time_step * w
 
-    def slopes(block, level):
-        r0 = pl.multiple_of(TOP + block * SUB, SUB)
-        at = pl.ds(r0, SUB)
-        for q, s, n in ((q_side, slope_side, 4), (q_main, slope_main, channels)):
-            if n == 4 and level == SUBSTEPS - 1:
-                continue
-            q = q.at[level % 2]
-            for k in range(n):
-                s[k, at, :] = half_minmod(rows_at(q, k, r0 - 1), rows_at(q, k, r0), rows_at(q, k, r0 + 1))
+    def row_of(block):
+        return pl.multiple_of(TOP + block * SUB, SUB)
+
+    def slopes_of(q, s, n, block):
+        r0 = row_of(block)
+        for k in range(n):
+            s[k, pl.ds(r0, SUB), :] = half_minmod(rows_at(q, k, r0 - 1), rows_at(q, k, r0), rows_at(q, k, r0 + 1))
 
     def row_fluxes(q, s, f, static, n, r0):
         lefts = [rows_at(q, k, r0) + rows_at(s, k, r0) for k in range(n)]
@@ -314,18 +325,21 @@
         out = face_fluxes(lefts, rights, 1, rows_at(static, 2, r0))
         for k in range(n):
             f[k, pl.ds(r0, SUB), :] = out[k]
-        return [rows_at(f, k, r0 - 1) - out[k] for k in range(n)]
-
-    def col_fluxes(here, static, n, r0, edges):
-        lefts, rights = [], []
+
+    def col_states(here, n, low, high, block, edges):
+        at = pl.ds(row_of(block), SUB)
         for k in range(n):
             before, after = pltpu.roll(here[k], 1, 1), pltpu.roll(here[k], LANES - 1, 1)
             if edges is not None:
                 before = jnp.where(first_lane, low_edge(edges[min(k, 3)], k), before)
                 after = jnp.where(last_lane, high_edge(edges[min(k, 3)], k), after)
             s = half_minmod(before, here[k], after)
-            lefts.append(here[k] + s)
-            rights.append(pltpu.roll(here[k] - s, LANES - 1, 1))
+            low[k, at, :] = here[k] + s
+            high[k, at, :] = here[k] - s
+
+    def col_fluxes(low, high, static, n, r0):
+        lefts = [rows_at(low, k, r0) for k in range(n)]
+        rights = [pltpu.roll(rows_at(high, k, r0), LANES - 1, 1) for k in range(n)]
         return face_fluxes(lefts, rights, 2, rows_at(static, 3, r0))
 
     def update(here, net, static, coeffs, r0):
@@ -333,7 +347,7 @@
         inv = pl.reciprocal(jnp.maximum(here[0], depth_floor))
         u, v = here[1] * inv, here[2] * inv
         squared = u * u + v * v + 1e-06
-        drag = drag_coeff * jnp.sqrt(squared)
+        drag = drag_coeff * (squared * lax.rsqrt(squared))
         new = [
             here[0] + step * net[0],
             here[1] + step * (net[1] - here[0] * rows_at(static, 4, r0) - drag * u),
@@ -342,72 +356,132 @@
         changes = []
         for k in range(len(here) - 3):
             m = here[3 + k]
-            settle, inv_critical, erode = coeffs[k]
-            change = step * (settle * m * inv - erode * jnp.maximum(squared * inv_critical - 1.0, 0.0))
+            settle, rate, erode = coeffs[k]
+            change = step * (settle * m * inv - jnp.maximum(squared * rate - erode, 0.0))
             changes.append(change)
             new.append(m + step * net[3 + k] - change)
         return new, changes
 
-    def advance(block, level, rows_only=False):
-        r0 = pl.multiple_of(TOP + block * SUB, SUB)
+
+    def slopes(block, level):
+        slopes_of(q_main[level % 2], slope_main, channels, block)
+        if level < SUBSTEPS - 1:
+            slopes_of(q_side[level % 2], slope_side, 4, block)
+
+    def states(block, level):
+        r0 = row_of(block)
+        edges = [rows_at(q_side[level % 2], k, r0) for k in range(4)]
+        here = [rows_at(q_main[level % 2], k, r0) for k in range(channels)]
+        col_states(edges, 4, low_side, high_side, block, None)
+        col_states(here, channels, low_main, high_main, block, edges)
+
+    def row_faces(block, level):
+        r0 = row_of(block)
+        row_fluxes(q_main[level % 2], slope_main, flux_main, static_main, channels, r0)
+        if level < SUBSTEPS - 1:
+            row_fluxes(q_side[level % 2], slope_side, flux_side, static_side, 4, r0)
+
+    def faces(block, level):
+        r0 = row_of(block)
+        row_faces(block, level)
+        for cross, low, high, static, n in (
+            (cross_side, low_side, high_side, static_side, 4), (cross_main, low_main, high_main, static_main, channels),
+        ):
+            for k, f in enumerate(col_fluxes(low, high, static, n, r0)):
+                cross[k, pl.ds(r0, SUB), :] = f
+
+    def finish(block, level):
+        r0 = row_of(block)
         at = pl.ds(r0, SUB)
-        last = level == SUBSTEPS - 1
-        qs, qm = q_side.at[level % 2], q_main.at[level % 2]
-        slopes(block + 1, level)
-        if rows_only:
-            row_fluxes(qm, slope_main, flux_main, static_main, channels, r0)
-            if not last:
-                row_fluxes(qs, slope_side, flux_side, static_side, 4, r0)
-            return
-        edges = [rows_at(qs, k, r0) for k in range(4)]
-        side_flux = col_fluxes(edges, static_side, 4, r0, None)
-        if not last:
-            net = row_fluxes(qs, slope_side, flux_side, static_side, 4, r0)
-            net = [x + (pltpu.roll(f, 1, 1) - f) for x, f in zip(net, side_flux)]
-            new, _ = update(edges, net, static_side, [coeffs_of(fractions)], r0)
+        edges = [rows_at(cross_side, k, r0) for k in range(4)]
+
+        def net_of(flux, k, cross, before):
+            return (rows_at(flux, k, r0 - 1) - rows_at(flux, k, r0)) + (before - cross)
+
+        if level < SUBSTEPS - 1:
+            q = q_side[level % 2]
+            net = [net_of(flux_side, k, edges[k], pltpu.roll(edges[k], 1, 1)) for k in range(4)]
+            new, _ = update([rows_at(q, k, r0) for k in range(4)], net, static_side, [coeffs_of(fractions)], r0)
             for k in range(4):
-                q_side[(level + 1) % 2, k, at, :] = new[k]
-        net = row_fluxes(qm, slope_main, flux_main, static_main, channels, r0)
-        here = [rows_at(qm, k, r0) for k in range(channels)]
-        fluxes = col_fluxes(here, static_main, channels, r0, edges)
+                q_side[(level + 1) % 2][k, at, :] = new[k]
+        net = []
         for k in range(channels):
-            edge = side_flux[min(k, 3)]
-            f = jnp.where(last_lane, turn(edge, LANES - 3 * RIM - start_of(k)), fluxes[k])
-            net[k] = net[k] + (jnp.where(first_lane, low_edge(edge, k), pltpu.roll(fluxes[k], 1, 1)) - f)
+            edge = edges[min(k, 3)]
+            f = rows_at(cross_main, k, r0)
+            before = jnp.where(first_lane, low_edge(edge, k), pltpu.roll(f, 1, 1))
+            f = jnp.where(last_lane, turn(edge, LANES - 3 * RIM - start_of(k)), f)
+            net.append(net_of(flux_main, k, f, before))
+        here = [rows_at(q_main[level % 2], k, r0) for k in range(channels)]
         new, changes = update(here, net, static_main, [coeffs_of(k) for k in range(fractions)], r0)
         for k in range(channels):
-            q_main[(level + 1) % 2, k, at, :] = new[k]
+            q_main[(level + 1) % 2][k, at, :] = new[k]
         for k in range(fractions):
             if level == 0:
                 exchanged[k, at, :] = changes[k]
             else:
                 exchanged[k, at, :] = exchanged[k, at, :] + changes[k]
 
-    def sweep(first, end, level, unroll=None):
-        def one(block, carry):
-            advance(block, level)
+    def first_fluxes(block, level):
+        slopes(block, level)
+        slopes(block + 1, level)
+        row_faces(block, level)
+
+    def each(blocks, level):
+        for block in sorted({*blocks, *(b + 1 for b in blocks)}):
+            slopes(block, level)
+        for stage in (states, faces, finish):
+            for block in blocks:
+                stage(block, level)
+
+    def sweep(first, end, level):
+        size = GROUP if (end - first) % GROUP == 0 else 1
+        if end - first <= STRAIGHT or end - first < 3 * size:
+            return each(list(range(first, end)), level)
+
+        def of(start):
+            return [start + n for n in range(size)]
+
+        def trip(start, carry, ahead=2):
+            for block in of(start):
+                finish(block, level)
+            for block in of(start + 2 * size)[: size if ahead == 2 else ahead]:
+                slopes(block, level)
+            if ahead:
+                for block in of(start + size):
+                    faces(block, level)
+            if ahead == 2:
+                for block in of(start + 2 * size):
+                    states(block, level)
             return carry
 
-        if unroll is None:
-            for block in range(first, end):
-                advance(block, level)
-        else:
-            lax.fori_loop(first, end, one, 0, unroll=unroll)
-
-    return statics, slopes, advance, sweep
+        for block in range(first, first + 2 * size):
+            slopes(block, level)
+        for block in of(first):
+            states(block, level)
+        for block in of(first):
+            faces(block, level)
+        for block in of(first + size):
+            states(block, level)
+        trips = (end - first) // size
+        lax.fori_loop(0, trips - 2, lambda n, c: trip(first + n * size, c), 0)
+        trip(end - 2 * size, 0, ahead=1)
+        trip(end - size, 0, ahead=0)
+
+    return statics, first_fluxes, each, sweep
 
 
 def early_kernel(
     geometry, planes, packs, frame_ref, send_a, send_b, ends, coeffs,
-    q_main, q_side, static_main, static_side, flux_main, flux_side, exchanged, code, slope_main, slope_side,
+    q_main_a, q_main_b, q_side_a, q_side_b, static_main, static_side, flux_main, flux_side, exchanged, code, *work,
 ):
+    q_main, q_side = (q_main_a, q_main_b), (q_side_a, q_side_b)
     count, rows = planes.shape[:2]
     channels = count - 2
     body = TOP + RIM
     parity = lax.axis_index("row") % 2
     blocks = rows // SUB
     for k in range(channels):
-        q_main[0, k, pl.ds(body, rows), :] = planes[k]
+        q_main[0][k, pl.ds(body, rows), :] = planes[k]
     static_main[0, pl.ds(body, rows), :] = planes[channels]
     for block, is_first in ((0, True), (blocks - 1, False)):
         at = pl.ds(body + block * SUB, SUB)
@@ -416,42 +490,45 @@
         ]
         static_main[1, at, :] = mine[0]
         for k in range(4):
-            q_side[0, k, at, :] = mine[1 + k]
+            q_side[0][k, at, :] = mine[1 + k]
         static_side[0, at, :] = mine[5]
         static_side[1, at, :] = mine[6]
-        code[pl.ds(block * SUB, SUB), :] = ends[0 if is_first else 1]
+        code[pl.ds(SUB + block * SUB, SUB), :] = ends[0 if is_first else 1]
+    nowhere = jnp.full((SUB, LANES), -1, jnp.int32)
+    code[pl.ds(0, SUB), :] = nowhere
+    code[pl.ds(SUB + rows, SUB), :] = nowhere
     make = side_maker(geometry, planes, packs, frame_ref)
     for block in range(1, blocks - 1):
         at = pl.ds(body + block * SUB, SUB)
         sides, bed, coded = make(block)
         static_main[1, at, :] = bed
         for k in range(4):
-            q_side[0, k, at, :] = sides[k]
+            q_side[0][k, at, :] = sides[k]
         static_side[0, at, :] = sides[4]
         static_side[1, at, :] = sides[5]
-        code[pl.ds(block * SUB, SUB), :] = coded
-    statics, slopes, advance, sweep = stepper(
-        coeffs, q_main, q_side, static_main, static_side, slope_main, slope_side, flux_main, flux_side, exchanged
+        code[pl.ds(SUB + block * SUB, SUB), :] = coded
+    statics, first_fluxes, each, sweep = stepper(
+        coeffs, q_main, q_side, static_main, static_side, flux_main, flux_side, exchanged, *work
     )
     total = blocks + 2
     for block in range(1, total - 2):
         statics(block)
     for level in range(AHEAD):
-        slopes(1 + level, level)
-        advance(1 + level, level, rows_only=True)
-        sweep(2 + level, total - 2 - level, level, UNROLL)
+        first_fluxes(1 + level, level)
+        sweep(2 + level, total - 2 - level, level)
 
 
 def late_kernel(
     band_cols, recv_a, recv_b, coeffs, code,
-    q_main_in, q_side_in, static_main_in, static_side_in, flux_main_in, flux_side_in, exchanged_in,
+    q_in_0, q_in_1, q_in_2, q_in_3, static_main_in, static_side_in, flux_main_in, flux_side_in, exchanged_in,
     depth_out, flow_out, mud_out, partial,
-    q_main, q_side, static_main, static_side, flux_main, flux_side, exchanged,
-    slope_main, slope_side, sems,
+    q_main_a, q_main_b, q_side_a, q_side_b, static_main, static_side, flux_main, flux_side, exchanged,
+    sems, *work,
 ):
-    del q_main_in, q_side_in, static_main_in, static_side_in, flux_main_in, flux_side_in, exchanged_in
-    rows = code.shape[0]
-    channels = q_main.shape[1]
+    q_main, q_side = (q_main_a, q_main_b), (q_side_a, q_side_b)
+    del q_in_0, q_in_1, q_in_2, q_in_3, static_main_in, static_side_in, flux_main_in, flux_side_in, exchanged_in
+    rows = code.shape[0] - 2 * SUB
+    channels = q_main[0].shape[0]
     fractions = channels - 3
     body = TOP + RIM
     parity = lax.axis_index("row") % 2
@@ -465,34 +542,31 @@
     for k in range(channels + 8):
         def put(at, x, k=k):
             if k < channels:
-                q_main[0, k, at, :] = x
+                q_main[0][k, at, :] = x
             elif k < channels + 2:
                 static_main[k - channels, at, :] = x
             elif k < channels + 6:
-                q_side[0, k - channels - 2, at, :] = x
+                q_side[0][k - channels - 2, at, :] = x
             else:
                 static_side[k - channels - 6, at, :] = x
 
         fill(put, k)
-    statics, slopes, advance, sweep = stepper(
-        coeffs, q_main, q_side, static_main, static_side, slope_main, slope_side, flux_main, flux_side, exchanged
+    statics, first_fluxes, each, sweep = stepper(
+        coeffs, q_main, q_side, static_main, static_side, flux_main, flux_side, exchanged, *work
     )
     for block in (0, total - 2, total - 1):
         statics(block)
     if total > 3:
         statics(1)
     for level in range(SUBSTEPS):
-        slopes(0, level)
         if level < AHEAD:
-            sweep(0, 2 + level, level)
-            slopes(total - 2 - level, level)
-            sweep(total - 2 - level, total, level)
+            each([*range(2 + level), *range(total - 2 - level, total)], level)
         elif level < SUBSTEPS - 1:
-            sweep(0, total, level, UNROLL)
+            sweep(0, total, level)
         else:
-            advance(0, level, rows_only=True)
-            sweep(1, total - 1, level, UNROLL)
-    final = q_main.at[SUBSTEPS % 2]
+            first_fluxes(0, level)
+            sweep(1, total - 1, level)
+    final = q_main[SUBSTEPS % 2]
     here = pl.ds(body, rows)
     copies = [pltpu.make_async_copy(final.at[0, here], depth_out, sems.at[0])]
     copies.append(pltpu.make_async_copy(final.at[pl.ds(1, 2), here], flow_out, sems.at[1]))
@@ -501,8 +575,10 @@
         copy.start()
 
     coarse_rows = rows // 4
-    parts = [[exchanged[f, pl.ds(body + k, coarse_rows, stride=4), :] for k in range(4)] for f in range(fractions)]
-    codes = [code[pl.ds(k, coarse_rows, stride=4), :] for k in range(4)]
+    def apart(ref, first, row_shift):
+        return [ref[pl.ds(first - 4 * row_shift + k, coarse_rows, stride=4), :] for k in range(4)]
+
+    codes = [apart(code, SUB, row_shift - 1) for row_shift in range(3)]
     to_coarse = (
         lax.broadcasted_iota(jnp.int32, (LANES, LANES), 0) // 4 == lax.broadcasted_iota(jnp.int32, (LANES, LANES), 1)
     ).astype(jnp.bfloat16)
@@ -511,18 +587,14 @@
     for col_shift in range(7):
         sums = [None] * fractions
         for row_shift in range(3):
-            hits = [c == row_shift * 7 + col_shift for c in codes]
+            hits = [c == row_shift * 7 + col_shift for c in codes[row_shift]]
             for f in range(fractions):
-                part = None
-                for k in range(4):
-                    x = jnp.where(hits[k], parts[f][k], 0.0)
-                    part = x if part is None else part + x
-                if row_shift != 1:
-                    part = pltpu.roll(part, 1 if row_shift == 2 else coarse_rows - 1, 0)
-                sums[f] = part if sums[f] is None else sums[f] + part
+                for hit, x in zip(hits, apart(exchanged.at[f], body, row_shift - 1)):
+                    x = jnp.where(hit, x, 0.0)
+                    sums[f] = x if sums[f] is None else sums[f] + x
         rest = jnp.concatenate(sums, axis=0)
         z = None
-        for _ in range(3):
+        for _ in range(2):
             term = rest.astype(jnp.bfloat16)
             rest = rest - term.astype(jnp.float32)
             moved = jnp.dot(term, to_coarse, preferred_element_type=jnp.float32)
@@ -614,14 +686,16 @@
 
     span = tile_rows + 2 * RIM + 3 * SUB
     state = (
-        f32((2, channels, span, LANES)), f32((2, 4, span, LANES)), f32((7, span, LANES)), f32((7, span, LANES)),
+        f32((channels, span, LANES)), f32((channels, span, LANES)), f32((4, span, LANES)), f32((4, span, LANES)),
+        f32((7, span, LANES)), f32((7, span, LANES)),
         f32((channels, span, LANES)), f32((4, span, LANES)), f32((fractions, span, LANES)),
     )
-    slope_space = [space((channels, span, LANES)), space((4, span, LANES))]
+    main_space, side_space = space((channels, span, LANES)), space((4, span, LANES))
+    work_space = [main_space, side_space, main_space, main_space, side_space, side_space, main_space, side_space]
     *begun, code = pl.pallas_call(
         functools.partial(early_kernel, geometry),
-        out_shape=(*state, jax.ShapeDtypeStruct((tile_rows, LANES), jnp.int32)),
-        in_specs=[vmem()] * 7, out_specs=(vmem(),) * 8, compiler_params=params_of(), scratch_shapes=slope_space,
+        out_shape=(*state, jax.ShapeDtypeStruct((tile_rows + 2 * SUB, LANES), jnp.int32)),
+        in_specs=[vmem()] * 7, out_specs=(vmem(),) * 10, compiler_params=params_of(), scratch_shapes=work_space,
     )(planes, packs, framed, send_a, send_b, ends, coeffs)
     depth_out, discharge_out, sediment_out, partial = pl.pallas_call(
         functools.partial(late_kernel, band_cols),
@@ -629,9 +703,9 @@
             f32(water_depth.shape), f32(discharge.shape), f32(sediment.shape), f32((fractions * band_rows, LANES)),
             *state,
         ),
-        in_specs=[vmem()] * 11, out_specs=(hbm(),) * 3 + (vmem(),) * 8, compiler_params=params_of(),
-        input_output_aliases={4 + k: 4 + k for k in range(7)},
-        scratch_shapes=[*slope_space, pltpu.SemaphoreType.DMA((3,))],
+        in_specs=[vmem()] * 13, out_specs=(hbm(),) * 3 + (vmem(),) * 10, compiler_params=params_of(),
+        input_output_aliases={4 + k: 4 + k for k in range(9)},
+        scratch_shapes=[pltpu.SemaphoreType.DMA((3,)), *work_space],
     )(recv_a, recv_b, coeffs, code, *begun)[:4]
 
     sums = lax.all_gather(partial, "col", axis=0)

time: 31.4 us -> 27.8 us (0.89)
  Pallas kernels: 13.9 us -> 10.5 us
  waiting for transfers between devices: 0.54 us -> 0.15 us
    pallas_call x1, Pallas kernels: 8.29 us -> 4.53 us  [local(): pl.pallas_call(functools.partial(late_kernel, band_cols), out_shape=(f32(...]
    ppermute x1, waiting for transfers between devices: 0.53 us -> 0.15 us  [local(): recv_b = lax.ppermute(send_b, 'row', pairs_b)]
    pallas_call x1, Pallas kernels: 3.29 us -> 3.67 us  [local(): pl.pallas_call(functools.partial(early_kernel, geometry), out_shape=(*sta...]
  transfers between devices with their start and end apart: 2 -> 2, of which waited for: 1 -> 1; matrix products, arithmetic and copies ran while one was open for 0% -> 0% of each run, Pallas kernels for 10% -> 13%
where the time goes in v3:
time: 27.8 us; the launch traced here: 27.5 us
  blocking collectives  12.9 us (46%)
  Pallas kernels  10.5 us (38%)
  starting transfers between devices  3.31 us (12%)
  between operations  0.68 us (2%)
    all_gather x1, blocking collectives, local(): sums = lax.all_gather(partial, 'col', axis=0)  6.85 us
    all_gather x1, blocking collectives, local(): packs = lax.all_gather(packed, 'col', axis=0)  6.02 us
    pallas_call x1, Pallas kernels, local(): pl.pallas_call(functools.partial(late_kernel, band_cols), out_shape=(f32(...  4.53 us
    pallas_call x1, Pallas kernels, local(): pl.pallas_call(functools.partial(early_kernel, geometry), out_shape=(*sta...  3.67 us
    ppermute x1, starting transfers between devices, local(): recv_b = lax.ppermute(send_b, 'row', pairs_b)  2.01 us
    ppermute x1, starting transfers between devices, local(): recv_a = lax.ppermute(send_a, 'row', pairs_a)  1.3 us
    pallas_call x1, Pallas kernels, local(): pl.pallas_call(pack_kernel, out_shape=(f32((count, tile_rows, LANES)), f3...  1.24 us
    pallas_call x1, Pallas kernels, local(): pl.pallas_call(functools.partial(bed_kernel, geometry), out_shape=(f32((s...  0.75 us
  transfers between devices with their start and end apart: 2, of which 1 were waited for; matrix products, arithmetic and copies ran while one was open for 0% of the time, Pallas kernels for 13%

profile of v3, /device:TPU:25, one launch (start us, length us, event | category | flops | bytes accessed | tf_op | source)
XLA Modules:
  0.0 27.5 jit_solution(8515689252969190339)
XLA Ops:
  0.6 1.2 %shard_map.118 = (f32[9,64,128]{2,1,0:T(8,128)S(1)}, f32[3,5,8,128]{3,2,1,0:T(8,128)S(1)}, f32[80,128]{1,0:T(8,128)S(1)}) custom-call(f32[64,128]{1,0:T(8,128)} %depth.1, f32[2,64,128]{2,1,0:T(8,128)} %flow.1, f32[4,64,128]{2,1,0:T(8,128)} %mud.1, s32[64,128]{1,0:T(8,128)} %wet.1, s32[64,128]{1,0:T(8,128)} %cells.1, f32[4,128]{1,0:T(4,128)} %strip.1, ...), custom_call_target="tpu_custom_call" | custom-call | tf_op jit(solution)/shard_map/pallas_call | solution.py:653
  1.9 6.0 %all-gather = f32[320,128]{1,0:T(8,128)S(1)} all-gather(f32[80,128]{1,0:T(8,128)S(1)} %get-tuple-element.31), channel_id=2, replica_groups=mesh['row'=8,'col'=4] {'col'}, dimensions={0}, use_global_device_ids=true | all-gather | bytes 204800 | tf_op jit(solution)/shard_map/all_gather | solution.py:664
  7.9 0.3 %shard_map.119 = (f32[15,8,128]{2,1,0:T(8,128)S(1)}, f32[15,8,128]{2,1,0:T(8,128)S(1)}, s32[2,8,128]{2,1,0:T(8,128)S(1)}, f32[32,128]{1,0:T(8,128)S(1)}) custom-call(f32[9,64,128]{2,1,0:T(8,128)S(1)} %get-tuple-element.30.planes, f32[4,80,128]{2,1,0:T(8,128)S(1)} %bitcast.2), custom_call_target="tpu_custom_call" | custom-call | tf_op jit(solution)/shard_map/pallas_call | solution.py:673
  8.2 1.3 %collective-permute-start = (f32[15,8,128]{2,1,0:T(8,128)S(1)}, f32[15,8,128]{2,1,0:T(8,128)S(1)}, u32[]{:S(2)}, u32[]{:S(2)}) collective-permute-start(f32[15,8,128]{2,1,0:T(8,128)S(1)} %get-tuple-element.32.send_a), channel_id=1, source_target_pairs={{0,4},{4,0},{8,12},{12,8},{16,20},{20,16},{24,28},{28,24},{1,5},{5... | collective-permute-start | bytes 184328 | tf_op jit(solution)/shard_map/ppermute | solution.py:684
  9.5 2.0 %collective-permute-start.1 = (f32[15,8,128]{2,1,0:T(8,128)S(1)}, f32[15,8,128]{2,1,0:T(8,128)S(1)}, u32[]{:S(2)}, u32[]{:S(2)}) collective-permute-start(f32[15,8,128]{2,1,0:T(8,128)S(1)} %get-tuple-element.33.send_b), channel_id=1, source_target_pairs={{4,8},{8,4},{12,16},{16,12},{20,24},{24,20},{5,9},{9,5},{13,17},{1... | collective-permute-start | bytes 184328 | tf_op jit(solution)/shard_map/ppermute | solution.py:685
  11.5 3.7 %shard_map.120 = (f32[7,104,128]{2,1,0:T(8,128)S(1)}, f32[7,104,128]{2,1,0:T(8,128)S(1)}, f32[4,104,128]{2,1,0:T(8,128)S(1)}, f32[4,104,128]{2,1,0:T(8,128)S(1)}...) custom-call(f32[9,64,128]{2,1,0:T(8,128)S(1)} %get-tuple-element.30., ...), custom_call_target="tpu_custom_call" | custom-call | tf_op jit(solution)/shard_map/pallas_call | solution.py:695
  15.2 0.0 collective-permute-done.recv_a
  15.2 0.1 collective-permute-done.1.recv_b
  15.4 4.5 %shard_map.121 = (f32[64,128]{1,0:T(8,128)}, f32[2,64,128]{2,1,0:T(8,128)}, f32[4,64,128]{2,1,0:T(8,128)}, f32[64,128]{1,0:T(8,128)S(1)}, f32[7,104,128]{2,1,0:T...) custom-call(f32[15,8,128]{2,1,0:T(8,128)S(1)} %collective-permute-do, ...), custom_call_target="tpu_custom_call", output_to_operand_aliasing={{4}: (4, {}), {5}: (5, {}), {6}: (6, {}), {7}: (7, {}), {8}... | custom-call | tf_op jit(solution)/shard_map/pallas_call | solution.py:700
  19.9 6.8 %all-gather.1 = f32[256,128]{1,0:T(8,128)S(1)} all-gather(f32[64,128]{1,0:T(8,128)S(1)} %get-tuple-element.50), channel_id=3, replica_groups=mesh['row'=8,'col'=4] {'col'}, dimensions={0}, use_global_device_ids=true | all-gather | bytes 163840 | tf_op jit(solution)/shard_map/all_gather | solution.py:711
  26.8 0.8 %shard_map.122 = (f32[4,128]{1,0:T(4,128)}, f32[4,4,128]{2,1,0:T(4,128)}, f32[64,128]{1,0:T(8,128)}) custom-call(f32[4,64,128]{2,1,0:T(8,128)S(1)} %bitcast.4, f32[32,128]{1,0:T(8,128)S(1)} %get-tuple-element.35.frame_ref.bed, f32[9,64,128]{2,1,0:T(8,128)S(1)} %get-tuple-element.30.planes), custom_call_target="tpu_custom_call" | custom-call | tf_op jit(solution)/shard_map/pallas_call | solution.py:726
Async XLA Ops:
  8.2 7.0 %collective-permute-start = (f32[15,8,128]{2,1,0:T(8,128)S(1)}, f32[15,8,128]{2,1,0:T(8,128)S(1)}, u32[]{:S(2)}, u32[]{:S(2)}) collective-permute-start(f32[15,8,128]{2,1,0:T(8,128)S(1)} %get-tuple-element.32.send_a), channel_id=1, source_target_pairs={{0,4},{4,0},{8,12},{12,8},{16,20},{20,16},{24,28},{28,24},{1,5},{5... | collective-permute-start | bytes 184328 | tf_op jit(solution)/shard_map/ppermute | solution.py:684
  9.5 5.9 %collective-permute-start.1 = (f32[15,8,128]{2,1,0:T(8,128)S(1)}, f32[15,8,128]{2,1,0:T(8,128)S(1)}, u32[]{:S(2)}, u32[]{:S(2)}) collective-permute-start(f32[15,8,128]{2,1,0:T(8,128)S(1)} %get-tuple-element.33.send_b), channel_id=1, source_target_pairs={{4,8},{8,4},{12,16},{16,12},{20,24},{24,20},{5,9},{9,5},{13,17},{1... | collective-permute-start | bytes 184328 | tf_op jit(solution)/shard_map/ppermute | solution.py:685

commit v4 on v3

--- a/solution.py
+++ b/solution.py
@@ -7,12 +7,13 @@
 from jax.experimental.pallas import tpu as pltpu
 from jax.sharding import PartitionSpec as P
 
+
 SUBSTEPS = 4
 LANES = 128
 SUB = 8
 GROUP = 1
 STRAIGHT = 12
-AHEAD = 1
+AHEAD = 3
 TOP = SUB
 SMALLEST = 1.1754944e-38
 RIM = 2 * SUBSTEPS
@@ -29,10 +30,6 @@
 
 def vmem():
     return pl.BlockSpec(memory_space=pltpu.VMEM)
-
-
-def smem():
-    return pl.BlockSpec(memory_space=pltpu.SMEM)
 
 
 def lane_ids(shape):
@@ -118,12 +115,18 @@
         coeffs[c, fractions, :, :] = mixed
 
 
-def spread_rows(frame_ref, block, shift):
-    first = SUB + block * (SUB // 4) + shift
-    low = jnp.broadcast_to(frame_ref[pl.ds(first, 1), :], (SUB, LANES))
-    high = jnp.broadcast_to(frame_ref[pl.ds(first + 1, 1), :], (SUB, LANES))
-    sub = lax.broadcasted_iota(jnp.int32, (SUB, LANES), 0)
-    return jnp.where(sub < 4, low, high)
+WINDOW_LOW = 5
+WINDOW = LANES // 4 + 2 * WINDOW_LOW
+
+
+def fill_window(window_ref, frame_ref, first):
+    rows = window_ref.shape[0]
+    lane = lane_ids((rows, LANES))
+    parts = [
+        pltpu.roll(frame_ref[pl.ds(SUB - 1 + n, rows), :], (n * WINDOW - first + 2 * LANES) % LANES, 1)
+        for n in range(3)
+    ]
+    window_ref[...] = jnp.where(lane < WINDOW, parts[0], jnp.where(lane < 2 * WINDOW, parts[1], parts[2]))
 
 
 def split_cells(cells, band_cols):
@@ -136,11 +139,12 @@
     return cell_row - (block * (SUB // 4) + sub // 4)
 
 
-def lookup(frame_ref, block, shift, column):
-    found = pick(spread_rows(frame_ref, block, 0), column)
-    below = pick(spread_rows(frame_ref, block, -1), column)
-    above = pick(spread_rows(frame_ref, block, 1), column)
-    return jnp.where(shift == 0, found, jnp.where(shift < 0, below, above))
+def lookup(window_ref, block, shift, column):
+    first = block * (SUB // 4)
+    low = jnp.broadcast_to(window_ref[pl.ds(first, 1), :], (SUB, LANES))
+    high = jnp.broadcast_to(window_ref[pl.ds(first + 1, 1), :], (SUB, LANES))
+    sub = lax.broadcasted_iota(jnp.int32, (SUB, LANES), 0)
+    return pick(jnp.where(sub < 4, low, high), (shift + 1) * WINDOW + column)
 
 
 def starts_of(col_at, band_cols):
@@ -154,12 +158,12 @@
         frame_ref[pl.ds(SUB + r0, value.shape[0]), :] = value
 
 
-def side_maker(geometry, planes, packs, frame_ref):
+def side_maker(geometry, planes, packs, window_ref):
     band_cols, cols_count = geometry[:2]
     count, rows = planes.shape[:2]
     fractions = count - 5
     col_at = lax.axis_index("col")
-    coarse_start, frame_start = starts_of(col_at, band_cols)
+    coarse_start = starts_of(col_at, band_cols)[0]
     wet_at, cell_at = count - 2, count - 1
     pairs = LANES // (2 * RIM)
     lane = lane_ids((SUB, LANES))
@@ -175,39 +179,51 @@
     left = jnp.maximum(col_at - 1, 0)
     right = jnp.minimum(col_at + 1, cols_count - 1)
 
-    def make(block):
+    def gather_to(block, p, base):
         at = pl.ds(block * SUB, SUB)
-
-        def gather_to(p, base):
-            if p < pairs:
-                source, slot = at, p
-            else:
-                source = pl.ds(rows + ((p - pairs) * folded_rows(rows) + block // pairs) * SUB, SUB)
-                slot = block % pairs
-            x = planes[p, at, :]
-            low = turn(packs[left, source, :], base - 2 * RIM * slot - RIM)
-            high = turn(packs[right, source, :], base + 3 * RIM - 2 * RIM * slot)
-            own = jnp.where(is_first, turn(x, base + RIM), turn(x, base + 3 * RIM))
-            return jnp.where(is_low, low, jnp.where(is_high, high, own))
-
-        def for_all(p):
-            x = gather_to(p, 0)
-            x = jnp.where(lane < width, x, pltpu.roll(x, width, 1))
-            return jnp.where(lane < 2 * width, x, pltpu.roll(x, 2 * width, 1)) * scale
-
-        sides = [for_all(p) for p in range(3)]
-        each = gather_to(3, 0)
-        for k in range(1, fractions):
-            each = jnp.where(group == k, gather_to(3 + k, k * width), each)
-        sides.append(each * scale)
-        sides.append(for_all(wet_at))
-        side_row, side_col = split_cells(for_all(cell_at), band_cols)
-        side_at = jnp.where(scale > 0.0, side_col - frame_start, 0)
-        sides.append(lookup(frame_ref, block, row_shift_of(side_row, block), side_at) * scale)
-        cell_row, cell_col = split_cells(planes[cell_at, at, :], band_cols)
-        shift = row_shift_of(cell_row, block)
-        bed = lookup(frame_ref, block, shift, cell_col - frame_start)
-        return sides, bed, (shift + 1) * 7 + (cell_col - coarse_start - lane // 4 + 3)
+        if p < pairs:
+            source, slot = at, p
+        else:
+            source = pl.ds(rows + ((p - pairs) * folded_rows(rows) + block // pairs) * SUB, SUB)
+            slot = block % pairs
+        x = planes[p, at, :]
+        low = turn(packs[left, source, :], base - 2 * RIM * slot - RIM)
+        high = turn(packs[right, source, :], base + 3 * RIM - 2 * RIM * slot)
+        own = jnp.where(is_first, turn(x, base + RIM), turn(x, base + 3 * RIM))
+        return jnp.where(is_low, low, jnp.where(is_high, high, own))
+
+    def gathered(block, order):
+        out = gather_to(block, order[0], 0)
+        for k, p in enumerate(order[1:], 1):
+            out = jnp.where(group == k, gather_to(block, p, k * width), out)
+        return out * scale
+
+    def packed(block):
+        each = gathered(block, [3 + k for k in range(fractions)])
+        return each, gathered(block, (0, 1, 2, wet_at)), gathered(block, (cell_at,))
+
+    def cells_of(block, first_group):
+        cells = first_group
+        for k in range(1, LANES // width):
+            cells = jnp.where(group == k, pltpu.roll(first_group, k * width, 1), cells)
+        side_row, side_col = split_cells(cells, band_cols)
+        inside_grid = scale > 0.0
+        side_shift = jnp.where(inside_grid, row_shift_of(side_row, block), 0)
+        side_at = jnp.where(inside_grid, side_col - coarse_start + WINDOW_LOW, 0)
+        cell_row, cell_col = split_cells(planes[cell_at, pl.ds(block * SUB, SUB), :], band_cols)
+        return side_shift, side_at, row_shift_of(cell_row, block), cell_col - coarse_start
+
+    def beds(block, cells):
+        side_shift, side_at, shift, column = cells
+        side_bed = lookup(window_ref, block, side_shift, side_at) * scale
+        bed = lookup(window_ref, block, shift, column + WINDOW_LOW)
+        return side_bed, bed, (shift + 1) * 7 + (column - lane // 4 + 3)
+
+    def make(blocks):
+        first = [packed(block) for block in blocks]
+        second = [cells_of(block, x[2]) for block, x in zip(blocks, first)]
+        third = [beds(block, x) for block, x in zip(blocks, second)]
+        return [(each, shared, side_bed, bed, code) for (each, shared, _), (side_bed, bed, code) in zip(first, third)]
 
     return make
 
@@ -215,7 +231,7 @@
 def edge_kernel(geometry, planes, packs, *refs):
     _, cols_count, strip_rows, from_packs = geometry
     frame = None if from_packs else refs[0]
-    send_a, send_b, code, frame_ref = refs[0 if from_packs else 1 :]
+    send_a, send_b, code, frame_ref, window_ref = refs[0 if from_packs else 1 :]
     count, rows = planes.shape[:2]
     pairs = LANES // (2 * RIM)
     strip_at = rows + (count - pairs) * folded_rows(rows) * SUB
@@ -225,19 +241,21 @@
         )
     else:
         fill_frame(frame_ref, [(0, frame[...])])
-    make = side_maker(geometry, planes, packs, frame_ref)
+    coarse_start, frame_start = starts_of(lax.axis_index("col"), geometry[0])
+    fill_window(window_ref, frame_ref, coarse_start - frame_start - WINDOW_LOW)
+    make = side_maker(geometry, planes, packs, window_ref)
     parity = lax.axis_index("row") % 2
     last = rows // SUB - 1
-    done = [make(0), make(last)]
+    done = make((0, last))
     for out, turned in ((send_a, parity == 1), (send_b, parity == 0)):
-        for p in range(count + 6):
+        for p in range(count + 3):
             first, final = [
-                planes[p, pl.ds(b * SUB, SUB), :] if p < count - 1 else bed if p == count - 1 else sides[p - count]
-                for b, (sides, bed, _) in zip((0, last), done)
+                planes[p, pl.ds(b * SUB, SUB), :] if p < count - 1 else bed if p == count - 1 else (each, shared, side_bed)[p - count]
+                for b, (each, shared, side_bed, bed, _) in zip((0, last), done)
             ]
             out[p, :, :] = jnp.where(turned, first, final)
-    code[0, :, :] = done[0][2]
-    code[1, :, :] = done[1][2]
+    code[0, :, :] = done[0][4]
+    code[1, :, :] = done[1][4]
 
 
 def half_minmod(before, here, after):
@@ -274,6 +292,7 @@
     first_lane = lane == 0
     last_lane = lane == LANES - 1
     wet_at, bed_at = 0, 1
+    rim_block = (exchanged.shape[1] - 4 * SUB) // SUB
 
     def coeffs_of(k):
         return [coeffs[c, k, :, :] for c in range(3)]
@@ -415,7 +434,7 @@
         new, changes = update(here, net, static_main, [coeffs_of(k) for k in range(fractions)], r0)
         for k in range(channels):
             q_main[(level + 1) % 2][k, at, :] = new[k]
-        for k in range(fractions):
+        for k in range(fractions if 0 < block < rim_block else 0):
             if level == 0:
                 exchanged[k, at, :] = changes[k]
             else:
@@ -426,17 +445,30 @@
         slopes(block + 1, level)
         row_faces(block, level)
 
-    def each(blocks, level):
-        for block in sorted({*blocks, *(b + 1 for b in blocks)}):
-            slopes(block, level)
-        for stage in (states, faces, finish):
-            for block in blocks:
+    def each(work, meanwhile=()):
+        def all_slopes(some):
+            for block, level in sorted({*some, *((b + 1, n) for b, n in some)}):
+                slopes(block, level)
+
+        def run(stage, some):
+            for block, level in some:
                 stage(block, level)
+
+        all_slopes(work)
+        run(states, work)
+        run(faces, work)
+        if meanwhile:
+            first_fluxes(meanwhile[0][0] - 1, meanwhile[0][1])
+            all_slopes(meanwhile)
+            run(states, meanwhile)
+        run(finish, work)
+        run(faces, meanwhile)
+        run(finish, meanwhile)
 
     def sweep(first, end, level):
         size = GROUP if (end - first) % GROUP == 0 else 1
         if end - first <= STRAIGHT or end - first < 3 * size:
-            return each(list(range(first, end)), level)
+            return each([(block, level) for block in range(first, end)])
 
         def of(start):
             return [start + n for n in range(size)]
@@ -470,8 +502,20 @@
     return statics, first_fluxes, each, sweep
 
 
+def put_sides(q, static, at, each, shared, bed):
+    group = lane_ids(shared.shape) // (4 * RIM)
+    turned = [shared] + [pltpu.roll(shared, 4 * RIM * n, 1) for n in range(1, 4)]
+    for k, (ref, p) in enumerate(((q, 0), (q, 1), (q, 2), (static, 0))):
+        x = turned[(0 - k) % 4]
+        for g in range(1, 4):
+            x = jnp.where(group == g, turned[(g - k) % 4], x)
+        ref[p, at, :] = x
+    q[3, at, :] = each
+    static[1, at, :] = bed
+
+
 def early_kernel(
-    geometry, planes, packs, frame_ref, send_a, send_b, ends, coeffs,
+    geometry, planes, packs, window_ref, send_a, send_b, ends, coeffs,
     q_main_a, q_main_b, q_side_a, q_side_b, static_main, static_side, flux_main, flux_side, exchanged, code, *work,
 ):
     q_main, q_side = (q_main_a, q_main_b), (q_side_a, q_side_b)
@@ -486,26 +530,20 @@
     for block, is_first in ((0, True), (blocks - 1, False)):
         at = pl.ds(body + block * SUB, SUB)
         mine = [
-            jnp.where((parity == 1) == is_first, send_a[p], send_b[p]) for p in range(channels + 1, channels + 8)
+            jnp.where((parity == 1) == is_first, send_a[p], send_b[p]) for p in range(channels + 1, channels + 5)
         ]
         static_main[1, at, :] = mine[0]
-        for k in range(4):
-            q_side[0][k, at, :] = mine[1 + k]
-        static_side[0, at, :] = mine[5]
-        static_side[1, at, :] = mine[6]
+        put_sides(q_side[0], static_side, at, *mine[1:])
         code[pl.ds(SUB + block * SUB, SUB), :] = ends[0 if is_first else 1]
     nowhere = jnp.full((SUB, LANES), -1, jnp.int32)
     code[pl.ds(0, SUB), :] = nowhere
     code[pl.ds(SUB + rows, SUB), :] = nowhere
-    make = side_maker(geometry, planes, packs, frame_ref)
-    for block in range(1, blocks - 1):
+    make = side_maker(geometry, planes, packs, window_ref)
+    inner = range(1, blocks - 1)
+    for block, (each, shared, side_bed, bed, coded) in zip(inner, make(inner)):
         at = pl.ds(body + block * SUB, SUB)
-        sides, bed, coded = make(block)
         static_main[1, at, :] = bed
-        for k in range(4):
-            q_side[0][k, at, :] = sides[k]
-        static_side[0, at, :] = sides[4]
-        static_side[1, at, :] = sides[5]
+        put_sides(q_side[0], static_side, at, each, shared, side_bed)
         code[pl.ds(SUB + block * SUB, SUB), :] = coded
     statics, first_fluxes, each, sweep = stepper(
         coeffs, q_main, q_side, static_main, static_side, flux_main, flux_side, exchanged, *work
@@ -534,23 +572,13 @@
     parity = lax.axis_index("row") % 2
     total = rows // SUB + 2
 
-    def fill(put, p):
-        a, b = recv_a[p], recv_b[p]
-        put(pl.ds(TOP, RIM), jnp.where(parity == 1, a, b))
-        put(pl.ds(body + rows, RIM), jnp.where(parity == 1, b, a))
-
-    for k in range(channels + 8):
-        def put(at, x, k=k):
-            if k < channels:
-                q_main[0][k, at, :] = x
-            elif k < channels + 2:
-                static_main[k - channels, at, :] = x
-            elif k < channels + 6:
-                q_side[0][k - channels - 2, at, :] = x
-            else:
-                static_side[k - channels - 6, at, :] = x
-
-        fill(put, k)
+    for at, turned in ((pl.ds(TOP, RIM), parity == 1), (pl.ds(body + rows, RIM), parity == 0)):
+        came = [jnp.where(turned, recv_a[p], recv_b[p]) for p in range(channels + 5)]
+        for k in range(channels):
+            q_main[0][k, at, :] = came[k]
+        for k in range(2):
+            static_main[k, at, :] = came[channels + k]
+        put_sides(q_side[0], static_side, at, *came[channels + 2 :])
     statics, first_fluxes, each, sweep = stepper(
         coeffs, q_main, q_side, static_main, static_side, flux_main, flux_side, exchanged, *work
     )
@@ -558,14 +586,18 @@
         statics(block)
     if total > 3:
         statics(1)
-    for level in range(SUBSTEPS):
-        if level < AHEAD:
-            each([*range(2 + level), *range(total - 2 - level, total)], level)
-        elif level < SUBSTEPS - 1:
+
+    def outer(level):
+        return [(block, level) for block in (*range(2 + level), *range(total - 2 - level, total))]
+
+    each(outer(0), [(block, AHEAD) for block in range(2 + AHEAD, total - 2 - AHEAD)] if AHEAD < SUBSTEPS - 1 else ())
+    for level in range(1, SUBSTEPS - 1):
+        if level <= AHEAD:
+            each(outer(level))
+        else:
             sweep(0, total, level)
-        else:
-            first_fluxes(0, level)
-            sweep(1, total - 1, level)
+    first_fluxes(0, SUBSTEPS - 1)
+    sweep(1, total - 1, SUBSTEPS - 1)
     final = q_main[SUBSTEPS % 2]
     here = pl.ds(body, rows)
     copies = [pltpu.make_async_copy(final.at[0, here], depth_out, sems.at[0])]
@@ -575,6 +607,7 @@
         copy.start()
 
     coarse_rows = rows // 4
+
     def apart(ref, first, row_shift):
         return [ref[pl.ds(first - 4 * row_shift + k, coarse_rows, stride=4), :] for k in range(4)]
 
@@ -606,7 +639,7 @@
         copy.wait()
 
 
-def bed_kernel(geometry, sums, bed, planes, bed_out, deposit_out, fine, frame_ref, total_ref):
+def bed_kernel(geometry, sums, bed, planes, bed_out, deposit_out, fine, frame_ref, total_ref, window_ref):
     band_cols, cols_count, strip_rows = geometry
     cells = planes.at[planes.shape[0] - 1]
     rows = cells.shape[0]
@@ -625,10 +658,12 @@
         deposit_out[f, :, :] = total_ref[pl.ds(f * band_rows + at, strip_rows), :]
     frame_ref[pl.ds(SUB, band_rows), :] = bed[pl.ds(SUB, band_rows), :] + whole
     bed_out[...] = frame_ref[pl.ds(SUB + at, strip_rows), :]
+    coarse_start, frame_start = starts_of(lax.axis_index("col"), band_cols)
+    fill_window(window_ref, frame_ref, coarse_start - frame_start - WINDOW_LOW)
     for block in range(rows // SUB):
         here = pl.ds(block * SUB, SUB)
         cell_row, cell_col = split_cells(cells[here, :], band_cols)
-        fine[here, :] = lookup(frame_ref, block, row_shift_of(cell_row, block), cell_col)
+        fine[here, :] = lookup(window_ref, block, row_shift_of(cell_row, block), cell_col - coarse_start + WINDOW_LOW)
 
 
 def local(water_depth, discharge, sediment, bed_level, cell_map, wet_mask, sediment_params):
@@ -670,19 +705,20 @@
         wide = jnp.pad(band, ((0, 0), (LANES, LANES)))
         frames = [lax.dynamic_slice(wide, (jnp.int32(0), frame_start + LANES), (band_rows, LANES))]
     geometry = (band_cols, cols_count, strip_rows, narrow)
-    send_a, send_b, ends, framed = pl.pallas_call(
+    send_a, send_b, ends, framed, window = pl.pallas_call(
         functools.partial(edge_kernel, geometry),
         out_shape=(
-            f32((count + 6, SUB, LANES)), f32((count + 6, SUB, LANES)),
+            f32((count + 3, SUB, LANES)), f32((count + 3, SUB, LANES)),
             jax.ShapeDtypeStruct((2, SUB, LANES), jnp.int32), f32((band_rows + 2 * SUB, LANES)),
+            f32((band_rows, LANES)),
         ),
-        in_specs=[vmem()] * (2 + len(frames)), out_specs=(vmem(),) * 4, compiler_params=params_of(),
+        in_specs=[vmem()] * (2 + len(frames)), out_specs=(vmem(),) * 5, compiler_params=params_of(),
     )(planes, packs, *frames)
 
     pairs_a = [p for i in range(0, rows_count - 1, 2) for p in ((i, i + 1), (i + 1, i))]
     pairs_b = [p for i in range(1, rows_count - 1, 2) for p in ((i, i + 1), (i + 1, i))]
+    recv_b = lax.ppermute(send_b, "row", pairs_b)
     recv_a = lax.ppermute(send_a, "row", pairs_a)
-    recv_b = lax.ppermute(send_b, "row", pairs_b)
 
     span = tile_rows + 2 * RIM + 3 * SUB
     state = (
@@ -696,7 +732,7 @@
         functools.partial(early_kernel, geometry),
         out_shape=(*state, jax.ShapeDtypeStruct((tile_rows + 2 * SUB, LANES), jnp.int32)),
         in_specs=[vmem()] * 7, out_specs=(vmem(),) * 10, compiler_params=params_of(), scratch_shapes=work_space,
-    )(planes, packs, framed, send_a, send_b, ends, coeffs)
+    )(planes, packs, window, send_a, send_b, ends, coeffs)
     depth_out, discharge_out, sediment_out, partial = pl.pallas_call(
         functools.partial(late_kernel, band_cols),
         out_shape=(
@@ -709,10 +745,8 @@
     )(recv_a, recv_b, coeffs, code, *begun)[:4]
 
     sums = lax.all_gather(partial, "col", axis=0)
-    geometry = (band_cols if narrow else LANES, cols_count, strip_rows)
-    if narrow:
-        look_cells = planes
-    else:
+    geometry = (band_cols, cols_count, strip_rows)
+    if not narrow:
         wide = jnp.zeros((fractions, band_rows, band_cols + 2 * LANES), jnp.float32)
         for d in range(cols_count):
             start = LANES + d * (tile_cols // 4) - (LANES - tile_cols // 4) // 2
@@ -721,14 +755,15 @@
         deposit_wide = exner_factor / 16.0 * share
         bed_wide = bed_level + jnp.sum(deposit_wide, axis=0)
         sums = lax.dynamic_slice_in_dim(wide, frame_start + LANES, LANES, axis=2).reshape(1, -1, LANES)
-        geometry = (LANES, 1, strip_rows)
-        look_cells = (cell_map // band_cols * LANES + cell_map % band_cols - frame_start).astype(jnp.float32)[None]
+        geometry = (band_cols, 1, strip_rows)
     bed_new, deposit, fine_bed = pl.pallas_call(
         functools.partial(bed_kernel, geometry),
         out_shape=(f32((strip_rows, LANES)), f32((fractions, strip_rows, LANES)), f32((tile_rows, LANES))),
         in_specs=[vmem()] * 3, out_specs=(vmem(),) * 3, compiler_params=params_of(),
-        scratch_shapes=[space((band_rows + 2 * SUB, LANES)), space((fractions * band_rows, LANES))],
-    )(sums, framed, look_cells)
+        scratch_shapes=[
+            space((band_rows + 2 * SUB, LANES)), space((fractions * band_rows, LANES)), space((band_rows, LANES)),
+        ],
+    )(sums, framed, planes)
     if not narrow:
         bed_new, deposit = bed_wide, deposit_wide
     return (depth_out, discharge_out, sediment_out, fine_bed, bed_new, deposit)

time: 27.8 us -> 26.8 us (0.964)
  Pallas kernels: 10.5 us -> 8.14 us
  waiting for transfers between devices: 0.15 us -> 1.71 us
    pallas_call x1, Pallas kernels: 3.67 us -> 1.98 us  [local(): pl.pallas_call(functools.partial(early_kernel, geometry), out_shape=(*sta...]
    ppermute x1, waiting for transfers between devices: 0.15 us -> 1.7 us  [local(): recv_b = lax.ppermute(send_b, 'row', pairs_b)]
    pallas_call x1, Pallas kernels: 4.53 us -> 3.89 us  [local(): pl.pallas_call(functools.partial(late_kernel, band_cols), out_shape=(f32(...]
  transfers between devices with their start and end apart: 2 -> 2, of which waited for: 1 -> 1; matrix products, arithmetic and copies ran while one was open for 0% -> 0% of each run, Pallas kernels for 13% -> 7%
where the time goes in v4:
time: 26.8 us; the launch traced here: 26.7 us
  blocking collectives  12.9 us (48%)
  Pallas kernels  8.14 us (30%)
  starting transfers between devices  3.29 us (12%)
  waiting for transfers between devices  1.71 us (6%)
  between operations  0.68 us (3%)
    all_gather x1, blocking collectives, local(): sums = lax.all_gather(partial, 'col', axis=0)  6.85 us
    all_gather x1, blocking collectives, local(): packs = lax.all_gather(packed, 'col', axis=0)  6.02 us
    pallas_call x1, Pallas kernels, local(): pl.pallas_call(functools.partial(late_kernel, band_cols), out_shape=(f32(...  3.89 us
    ppermute x1, starting transfers between devices, local(): recv_b = lax.ppermute(send_b, 'row', pairs_b)  2.01 us
    pallas_call x1, Pallas kernels, local(): pl.pallas_call(functools.partial(early_kernel, geometry), out_shape=(*sta...  1.98 us
    ppermute x1, waiting for transfers between devices, local(): recv_b = lax.ppermute(send_b, 'row', pairs_b)  1.7 us
    ppermute x1, starting transfers between devices, local(): recv_a = lax.ppermute(send_a, 'row', pairs_a)  1.28 us
    pallas_call x1, Pallas kernels, local(): pl.pallas_call(pack_kernel, out_shape=(f32((count, tile_rows, LANES)), f3...  1.24 us
  transfers between devices with their start and end apart: 2, of which 1 were waited for; matrix products, arithmetic and copies ran while one was open for 0% of the time, Pallas kernels for 7%

profile of v4, /device:TPU:25, one launch (start us, length us, event | category | flops | bytes accessed | tf_op | source)
XLA Modules:
  0.0 26.7 jit_solution(14851871091243169994)
XLA Ops:
  0.6 1.2 %shard_map.118 = (f32[9,64,128]{2,1,0:T(8,128)S(1)}, f32[3,5,8,128]{3,2,1,0:T(8,128)S(1)}, f32[80,128]{1,0:T(8,128)S(1)}) custom-call(f32[64,128]{1,0:T(8,128)} %depth.1, f32[2,64,128]{2,1,0:T(8,128)} %flow.1, f32[4,64,128]{2,1,0:T(8,128)} %mud.1, s32[64,128]{1,0:T(8,128)} %wet.1, s32[64,128]{1,0:T(8,128)} %cells.1, f32[4,128]{1,0:T(4,128)} %strip.1, ...), custom_call_target="tpu_custom_call" | custom-call | tf_op jit(solution)/shard_map/pallas_call | solution.py:688
  1.9 6.0 %all-gather = f32[320,128]{1,0:T(8,128)S(1)} all-gather(f32[80,128]{1,0:T(8,128)S(1)} %get-tuple-element.32), channel_id=2, replica_groups=mesh['row'=8,'col'=4] {'col'}, dimensions={0}, use_global_device_ids=true | all-gather | bytes 204800 | tf_op jit(solution)/shard_map/all_gather | solution.py:699
  7.9 0.2 shard_map.119
  8.1 1.3 %collective-permute-start = (f32[12,8,128]{2,1,0:T(8,128)S(1)}, f32[12,8,128]{2,1,0:T(8,128)S(1)}, u32[]{:S(2)}, u32[]{:S(2)}) collective-permute-start(f32[12,8,128]{2,1,0:T(8,128)S(1)} %get-tuple-element.33.send_a), channel_id=1, source_target_pairs={{0,4},{4,0},{8,12},{12,8},{16,20},{20,16},{24,28},{28,24},{1,5},{5... | collective-permute-start | bytes 147464 | tf_op jit(solution)/shard_map/ppermute | solution.py:721
  9.4 2.0 %collective-permute-start.1 = (f32[12,8,128]{2,1,0:T(8,128)S(1)}, f32[12,8,128]{2,1,0:T(8,128)S(1)}, u32[]{:S(2)}, u32[]{:S(2)}) collective-permute-start(f32[12,8,128]{2,1,0:T(8,128)S(1)} %get-tuple-element.34.send_b), channel_id=1, source_target_pairs={{4,8},{8,4},{12,16},{16,12},{20,24},{24,20},{5,9},{9,5},{13,17},{1... | collective-permute-start | bytes 147464 | tf_op jit(solution)/shard_map/ppermute | solution.py:720
  11.4 2.0 %shard_map.120 = (f32[7,104,128]{2,1,0:T(8,128)S(1)}, f32[7,104,128]{2,1,0:T(8,128)S(1)}, f32[4,104,128]{2,1,0:T(8,128)S(1)}, f32[4,104,128]{2,1,0:T(8,128)S(1)}...) custom-call(f32[9,64,128]{2,1,0:T(8,128)S(1)} %get-tuple-element.31., ...), custom_call_target="tpu_custom_call" | custom-call | tf_op jit(solution)/shard_map/pallas_call | solution.py:731
  13.4 0.0 collective-permute-done.recv_a
  13.4 1.7 %collective-permute-done.1.recv_b = f32[12,8,128]{2,1,0:T(8,128)S(1)} collective-permute-done((f32[12,8,128]{2,1,0:T(8,128)S(1)}, f32[12,8,128]{2,1,0:T(8,128)S(1)}, u32[]{:S(2)}, u32[]{:S(2)}) %collective-permute-start.1) | collective-permute-done | bytes 49184 | tf_op jit(solution)/shard_map/ppermute | solution.py:720
  15.1 3.9 %shard_map.121 = (f32[64,128]{1,0:T(8,128)}, f32[2,64,128]{2,1,0:T(8,128)}, f32[4,64,128]{2,1,0:T(8,128)}, f32[64,128]{1,0:T(8,128)S(1)}, f32[7,104,128]{2,1,0:T...) custom-call(f32[12,8,128]{2,1,0:T(8,128)S(1)} %collective-permute-do, ...), custom_call_target="tpu_custom_call", output_to_operand_aliasing={{4}: (4, {}), {5}: (5, {}), {6}: (6, {}), {7}: (7, {}), {8}... | custom-call | tf_op jit(solution)/shard_map/pallas_call | solution.py:736
  19.0 6.8 %all-gather.1 = f32[256,128]{1,0:T(8,128)S(1)} all-gather(f32[64,128]{1,0:T(8,128)S(1)} %get-tuple-element.51), channel_id=3, replica_groups=mesh['row'=8,'col'=4] {'col'}, dimensions={0}, use_global_device_ids=true | all-gather | bytes 163840 | tf_op jit(solution)/shard_map/all_gather | solution.py:747
  25.9 0.8 %shard_map.122 = (f32[4,128]{1,0:T(4,128)}, f32[4,4,128]{2,1,0:T(4,128)}, f32[64,128]{1,0:T(8,128)}) custom-call(f32[4,64,128]{2,1,0:T(8,128)S(1)} %bitcast.4, f32[32,128]{1,0:T(8,128)S(1)} %get-tuple-element.52.bed, f32[9,64,128]{2,1,0:T(8,128)S(1)} %get-tuple-element.31.planes), custom_call_target="tpu_custom_call" | custom-call | tf_op jit(solution)/shard_map/pallas_call | solution.py:759
Async XLA Ops:
  8.1 5.3 %collective-permute-start = (f32[12,8,128]{2,1,0:T(8,128)S(1)}, f32[12,8,128]{2,1,0:T(8,128)S(1)}, u32[]{:S(2)}, u32[]{:S(2)}) collective-permute-start(f32[12,8,128]{2,1,0:T(8,128)S(1)} %get-tuple-element.33.send_a), channel_id=1, source_target_pairs={{0,4},{4,0},{8,12},{12,8},{16,20},{20,16},{24,28},{28,24},{1,5},{5... | collective-permute-start | bytes 147464 | tf_op jit(solution)/shard_map/ppermute | solution.py:721
  9.4 5.7 %collective-permute-start.1 = (f32[12,8,128]{2,1,0:T(8,128)S(1)}, f32[12,8,128]{2,1,0:T(8,128)S(1)}, u32[]{:S(2)}, u32[]{:S(2)}) collective-permute-start(f32[12,8,128]{2,1,0:T(8,128)S(1)} %get-tuple-element.34.send_b), channel_id=1, source_target_pairs={{4,8},{8,4},{12,16},{16,12},{20,24},{24,20},{5,9},{9,5},{13,17},{1... | collective-permute-start | bytes 147464 | tf_op jit(solution)/shard_map/ppermute | solution.py:720
